TPU v7x, 256 devices: a whole 4x4x8 slice. The times are simulated.
256 devices in a mesh: tile: 32 (over z_lo, y, core), depth: 8 (over z_hi, x).
Axes of the slice: x: 4, y: 4, z: 8 (z_hi: 2, z_lo: 4; z = z_hi * 4 + z_lo), core: 2. Of those that a mesh axis runs over, the one named last changes fastest.
Arguments:
- objects: float32 [8, 4, 4096, 256], P('depth', None, 'tile'), may hold values from 0.25 to 30, as said below
- observed: float32 [8, 4, 4096, 256], P('depth', None, 'tile'), may hold values from 0.25 to 30, as said below
- pupil_phase: float32 [8, 128, 128], P('depth'), may hold values from -319 to 319
- pupil_amplitude: float32 [8, 128, 128], P('depth'), may hold values from 0.25 to 1.75
Outputs:
- new_objects: float32 [8, 4, 4096, 256], P('depth', None, 'tile')
- new_phase: float32 [8, 128, 128], P('depth')
Inputs may be any that keep to these rules, and one draw needn't show every extreme that they name: `objects`: strictly positive intensities. `observed`: strictly positive intensities.
All inputs are finite; a program needn't handle non-finite values.
Results may differ from a plain program's by a relative error of at most 0.0001.
Values sent between devices are 32-bit elements; how exact they have to be, the bound alone decides.
A program may use at most 64 MiB of HBM per device.

v0:
```python
import math

import jax
import jax.numpy as jnp
import numpy as np
from jax import lax
from jax.experimental import pallas as pl
from jax.experimental.pallas import tpu as pltpu
from jax.sharding import PartitionSpec as P

HALF = 64
KER = 129
PUP = 128
PAD = 136
BACKGROUND = 0.1
STEP_SIZE = 0.3
EPSILON = 1e-06
MESH = pl.DeviceIdType.MESH


def real_form(matrix):
    return np.block([[matrix.real, matrix.imag], [-matrix.imag, matrix.real]])


def tables(rows, cols):
    span = rows + 2 * HALF
    half = span // 2
    omega = 2.0 * np.pi * (2.0 * np.arange(half) + 0.5) / span
    turn = np.exp(-1j * omega[:, None] * np.arange(span)[None, :])
    row_all = np.concatenate([turn.real, turn.imag])
    row_mid = row_all[:, HALF : HALF + rows]
    lag = np.exp(-1j * omega[:, None] * (np.arange(PAD) - HALF)[None, :]) * (np.arange(PAD) < KER)
    row_lag = np.concatenate([lag.real, lag.imag])
    part = cols // 2
    where = np.arange(part)
    even = np.exp(-2j * np.pi * where[:, None] * (2 * where)[None, :] / cols)
    odd = np.exp(-2j * np.pi * where[:, None] * (2 * where + 1)[None, :] / cols)
    shift_even = np.exp(2j * np.pi * HALF * 2 * where / cols)
    shift_odd = np.exp(2j * np.pi * HALF * (2 * where + 1) / cols)
    col = [real_form(even), real_form(odd)]
    col_lag = [real_form(even * shift_even), real_form(odd * shift_odd)]
    outs = np.arange(PAD)
    ring = np.exp(-2j * np.pi * (((outs - HALF)[:, None] * np.arange(PUP)[None, :]) % KER) / KER)
    ring = ring * (outs < KER)[:, None]
    left = np.block([[ring.real, -ring.imag], [ring.imag, ring.real]])
    wide = np.zeros((PUP, cols), complex)
    wide[:, :PAD] = ring.T
    right = real_form(wide)
    grid = np.arange(PUP) - (PUP - 1) / 2.0
    aperture = (grid[:, None] ** 2 + grid[None, :] ** 2 <= (PUP / 2.0) ** 2).astype(float)
    named = dict(
        row_all=row_all,
        row_mid=row_mid,
        row_back=row_mid.T * (2.0 / span),
        row_lag=row_lag,
        row_lag_back=row_lag.T * (2.0 / span),
        even=col[0],
        odd=col[1],
        even_back=col[0].T / cols,
        odd_back=col[1].T / cols,
        even_lag=col_lag[0],
        odd_lag=col_lag[1],
        even_lag_back=col_lag[0].T / cols,
        odd_lag_back=col_lag[1].T / cols,
        left=left,
        left_back=left.T,
        right=right,
        right_back=right.T,
        aperture=aperture,
    )
    return {name: np.ascontiguousarray(value, dtype=np.float32) for name, value in named.items()}


def fine(left, right):
    return jnp.dot(left, right, precision=lax.Precision.HIGHEST, preferred_element_type=jnp.float32)


def mm(left, right):
    return jnp.dot(left, right, precision=lax.Precision.HIGH, preferred_element_type=jnp.float32)


def sin_cos(angle):
    count = jnp.floor(angle * (2.0 / math.pi) + 0.5)
    rest = angle - count * 1.5703125
    rest = rest - count * 4.8375129699707031e-4
    rest = rest - count * 7.549789954891882e-8
    square = rest * rest
    sine = ((-1.9515295891e-4 * square + 8.3321608736e-3) * square - 1.6666654611e-1) * square * rest + rest
    cosine = (
        (2.443315711809948e-5 * square - 1.388731625493765e-3) * square + 4.166664568298827e-2
    ) * square * square - 0.5 * square + 1.0
    quarter = count - 4.0 * jnp.floor(count * 0.25)
    swap = (quarter == 1.0) | (quarter == 3.0)
    sin_out = jnp.where(swap, cosine, sine)
    cos_out = jnp.where(swap, sine, cosine)
    sin_out = jnp.where(quarter >= 2.0, -sin_out, sin_out)
    cos_out = jnp.where((quarter == 1.0) | (quarter == 2.0), -cos_out, cos_out)
    return sin_out, cos_out


def beside(one, two):
    return jnp.concatenate([one, two], axis=1)


def above(one, two):
    return jnp.concatenate([one, two], axis=0)


def split_cols(rowed):
    half = rowed.shape[0] // 2
    part = rowed.shape[1] // 2
    plus = rowed[:, :part] + rowed[:, part:]
    minus = rowed[:, :part] - rowed[:, part:]
    return beside(plus[:half], plus[half:]), beside(minus[:half], minus[half:])


def join_cols(even, odd):
    part = even.shape[1] // 2
    plus = even + odd
    minus = even - odd
    return above(
        beside(plus[:, :part], minus[:, :part]),
        beside(plus[:, part:], minus[:, part:]),
    )


def times(one, two):
    part = one.shape[1] // 2
    ar, ai, br, bi = one[:, :part], one[:, part:], two[:, :part], two[:, part:]
    return beside(ar * br - ai * bi, ar * bi + ai * br)


def times_conj(one, two):
    part = one.shape[1] // 2
    ar, ai, br, bi = one[:, :part], one[:, part:], two[:, :part], two[:, part:]
    return beside(ar * br + ai * bi, ai * br - ar * bi)


NAMES = (
    "row_all",
    "row_mid",
    "row_back",
    "row_lag",
    "row_lag_back",
    "even",
    "odd",
    "even_back",
    "odd_back",
    "even_lag",
    "odd_lag",
    "even_lag_back",
    "odd_lag_back",
    "left",
    "left_back",
    "right",
    "right_back",
    "aperture",
)


def kernel(tiles, depths, planes, rows, cols, *refs):
    obj, obs, phase_ref, amp_ref = refs[:4]
    t = dict(zip(NAMES, refs[4 : 4 + len(NAMES)]))
    out_obj, out_phase = refs[4 + len(NAMES) : 6 + len(NAMES)]
    (
        strip, rstrip, work_e, work_o, spec_e, spec_o, share, part, mine, full, sums,
        h1s, h1r, h2s, h2r, s1, r1, s2, r2, s3, r3,
    ) = refs[6 + len(NAMES) :]
    me = lax.axis_index("tile")
    layer = lax.axis_index("depth")
    span = rows + 2 * HALF
    half = span // 2
    barrier = pltpu.get_barrier_semaphore()
    for off in range(1, tiles):
        pl.semaphore_signal(barrier, 1, device_id={"tile": lax.rem(me + off, tiles)}, device_id_type=MESH)
    for off in range(1, depths):
        pl.semaphore_signal(barrier, 1, device_id={"depth": lax.rem(layer + off, depths)}, device_id_type=MESH)
    pl.semaphore_wait(barrier, tiles + depths - 2)

    def halo(source, source_row, buffer, sends, recvs, plane, direction):
        peer = lax.rem(me + (1 if direction == 0 else tiles - 1), tiles)
        start = source_row + (rows - HALF if direction == 0 else 0)
        target = 0 if direction == 0 else HALF + rows
        slot = 2 * plane + direction
        return pltpu.make_async_remote_copy(
            source.at[plane, pl.ds(start, HALF)], buffer.at[plane, pl.ds(target, HALF)],
            sends.at[slot], recvs.at[slot], device_id={"tile": peer}, device_id_type=MESH,
        )

    def halo1(plane, direction):
        return halo(obj, 0, strip, h1s, h1r, plane, direction)

    def halo2(plane, direction):
        return halo(rstrip, HALF, rstrip, h2s, h2r, plane, direction)

    for plane in range(planes):
        halo1(plane, 0).start()
        halo1(plane, 1).start()

    def spread_of(angle):
        sine, cosine = sin_cos(angle)
        weight = amp_ref[...] * t["aperture"][...]
        field = above(weight * cosine, weight * sine)
        lefts = fine(t["left"][...], field)
        outer = fine(beside(lefts[:PAD], lefts[PAD:]), t["right"][...])
        real, imag = outer[:, :cols], outer[:, cols:]
        intensity = real * real + imag * imag
        total = jnp.sum(intensity)
        return field, real, imag, total, intensity * (1.0 / total)

    def spectrum_of(psf):
        even, odd = split_cols(mm(t["row_lag"][...], psf))
        return mm(even, t["even_lag"][...]), mm(odd, t["odd_lag"][...])

    def forward(plane, rowed):
        even, odd = split_cols(rowed)
        at = pl.ds(plane * half, half)
        work_e[at] = even
        work_o[at] = odd

    def back(plane, even, odd):
        at = slice(plane * half, plane * half + half)
        return mm(t["row_back"][...], join_cols(even[at], odd[at]))

    def blurred(kernel_e, kernel_o):
        for plane in range(planes):
            at = pl.ds(plane * half, half)
            work_e[at] = times(spec_e[at], kernel_e)
            work_o[at] = times(spec_o[at], kernel_o)
        return mm(work_e[...], t["even_back"][...]), mm(work_o[...], t["odd_back"][...])

    phase = phase_ref[...]
    field, real, imag, total, psf = spread_of(phase)
    kernel_e, kernel_o = spectrum_of(psf)

    for plane in range(planes):
        strip[plane, pl.ds(HALF, rows)] = obj[plane]
    for plane in range(planes):
        halo1(plane, 0).wait()
        halo1(plane, 1).wait()
        forward(plane, mm(t["row_all"][...], strip[plane]))
    spec_e[...] = mm(work_e[...], t["even"][...])
    spec_o[...] = mm(work_o[...], t["odd"][...])

    even, odd = blurred(kernel_e, kernel_o)
    for plane in range(planes):
        misfit = 1.0 - obs[plane] / (back(plane, even, odd) + BACKGROUND)
        forward(plane, mm(t["row_mid"][...], misfit))
    mis_e = mm(work_e[...], t["even"][...])
    mis_o = mm(work_o[...], t["odd"][...])
    cross_e = jnp.zeros((half, cols), jnp.float32)
    cross_o = jnp.zeros((half, cols), jnp.float32)
    for plane in range(planes):
        at = slice(plane * half, plane * half + half)
        cross_e = cross_e + times_conj(mis_e[at], spec_e[at])
        cross_o = cross_o + times_conj(mis_o[at], spec_o[at])
    lagged = join_cols(fine(cross_e, t["even_lag_back"][...]), fine(cross_o, t["odd_lag_back"][...]))
    psf_grad = fine(t["row_lag_back"][...], lagged)

    scale = 2.0 / total
    centred = (psf_grad - jnp.sum(psf_grad * psf)) * scale
    lefts = fine(t["left_back"][...], above(centred * real, centred * imag))
    pupils = fine(beside(lefts[:PUP], lefts[PUP:]), t["right_back"][...])
    mygrad = field[:PUP] * pupils[:, PUP:] - field[PUP:] * pupils[:, :PUP]

    chunk = PUP // tiles
    for piece in range(tiles):
        share[piece] = mygrad[piece * chunk : (piece + 1) * chunk]

    def scatter(off):
        peer = lax.rem(me + off, tiles)
        return pltpu.make_async_remote_copy(
            share.at[peer], part.at[off - 1], s1.at[off - 1], r1.at[off - 1],
            device_id={"tile": peer}, device_id_type=MESH,
        )

    def gather(off):
        peer = lax.rem(me + off, tiles)
        return pltpu.make_async_remote_copy(
            mine, full.at[off - 1], s2.at[off - 1], r2.at[off - 1],
            device_id={"tile": peer}, device_id_type=MESH,
        )

    def spread(off):
        return pltpu.make_async_remote_copy(
            sums.at[0], sums.at[off], s3.at[off - 1], r3.at[off - 1],
            device_id={"depth": lax.rem(layer + off, depths)}, device_id_type=MESH,
        )

    for off in range(1, tiles):
        scatter(off).start()
    for off in range(1, tiles):
        scatter(off).wait()
    summed = share[me]
    for off in range(1, tiles):
        summed = summed + part[off - 1]
    mine[...] = summed
    for off in range(1, tiles):
        gather(off).start()
    for off in range(1, tiles):
        gather(off).wait()
    share[me] = summed
    for off in range(1, tiles):
        share[lax.rem(me + tiles - off, tiles)] = full[off - 1]
    gradient = jnp.concatenate([share[piece] for piece in range(tiles)], axis=0)
    sums[0] = jnp.broadcast_to(jnp.sum(gradient * gradient), (8, 128))
    for off in range(1, depths):
        spread(off).start()
    for off in range(1, depths):
        spread(off).wait()
    squares = sums[0]
    for off in range(1, depths):
        squares = squares + sums[off]
    mean_square = squares[0:1] * (1.0 / (depths * PUP * PUP))
    new_phase = phase - STEP_SIZE * gradient / jnp.sqrt(mean_square + EPSILON)
    out_phase[...] = new_phase

    _, _, _, _, psf = spread_of(new_phase)
    kernel_e, kernel_o = spectrum_of(psf)
    even, odd = blurred(kernel_e, kernel_o)
    for plane in range(planes):
        rstrip[plane, pl.ds(HALF, rows)] = obs[plane] / (back(plane, even, odd) + BACKGROUND)
        halo2(plane, 0).start()
        halo2(plane, 1).start()
    for plane in range(planes):
        halo2(plane, 0).wait()
        halo2(plane, 1).wait()
        forward(plane, mm(t["row_all"][...], rstrip[plane]))
    rat_e = mm(work_e[...], t["even"][...])
    rat_o = mm(work_o[...], t["odd"][...])
    for plane in range(planes):
        at = slice(plane * half, plane * half + half)
        work_e[pl.ds(plane * half, half)] = times_conj(rat_e[at], kernel_e)
        work_o[pl.ds(plane * half, half)] = times_conj(rat_o[at], kernel_o)
    even = mm(work_e[...], t["even_back"][...])
    odd = mm(work_o[...], t["odd_back"][...])
    for plane in range(planes):
        out_obj[plane] = obj[plane] * back(plane, even, odd)


def on_device(objects, observed, pupil_phase, pupil_amplitude):
    tiles, depths = lax.axis_size("tile"), lax.axis_size("depth")
    _, planes, rows, cols = objects.shape
    span = rows + 2 * HALF
    half = span // 2
    table = tables(rows, cols)
    f32 = jnp.float32
    vmem = pltpu.VMEM
    dma = pltpu.SemaphoreType.DMA
    chunk = PUP // tiles
    body = lambda *refs: kernel(tiles, depths, planes, rows, cols, *refs)
    new_objects, new_phase = pl.pallas_call(
        body,
        out_shape=(
            jax.ShapeDtypeStruct((planes, rows, cols), f32),
            jax.ShapeDtypeStruct((PUP, PUP), f32),
        ),
        in_specs=[pl.BlockSpec(memory_space=vmem)] * (4 + len(NAMES)),
        out_specs=(pl.BlockSpec(memory_space=vmem), pl.BlockSpec(memory_space=vmem)),
        scratch_shapes=[
            vmem((planes, span, cols), f32),
            vmem((planes, span, cols), f32),
            vmem((planes * half, cols), f32),
            vmem((planes * half, cols), f32),
            vmem((planes * half, cols), f32),
            vmem((planes * half, cols), f32),
            vmem((tiles, chunk, PUP), f32),
            vmem((tiles - 1, chunk, PUP), f32),
            vmem((chunk, PUP), f32),
            vmem((tiles - 1, chunk, PUP), f32),
            vmem((depths, 8, 128), f32),
            dma((2 * planes,)), dma((2 * planes,)), dma((2 * planes,)), dma((2 * planes,)),
            dma((tiles - 1,)), dma((tiles - 1,)), dma((tiles - 1,)), dma((tiles - 1,)),
            dma((depths - 1,)), dma((depths - 1,)),
        ],
        compiler_params=pltpu.CompilerParams(
            collective_id=0, has_side_effects=True, vmem_limit_bytes=48 * 1024 * 1024
        ),
        name="step",
    )(objects[0], observed[0], pupil_phase[0], pupil_amplitude[0], *[table[name] for name in NAMES])
    return new_objects[None], new_phase[None]


def solution(mesh):
    return jax.shard_map(
        on_device,
        mesh=mesh,
        in_specs=(
            P("depth", None, "tile", None),
            P("depth", None, "tile", None),
            P("depth", None, None),
            P("depth", None, None),
        ),
        out_specs=(P("depth", None, "tile", None), P("depth", None, None)),
        check_vma=False,
    )
```

profile of v0, /device:TPU:1, one launch (start us, length us, event | category | flops | bytes accessed | tf_op | source)
XLA Modules:
  0.0 72.2 jit_solution(15057451424452546408)
XLA Ops:
  0.6 0.0 copy-start
  0.6 1.0 %copy-done = f32[1,4,128,256]{3,2,1,0:T(8,128)S(1)} copy-done((f32[1,4,128,256]{3,2,1,0:T(8,128)S(1)}, f32[1,4,128,256]{3,2,1,0:T(8,128)}, u32[]{:S(2)}) %copy-start) | copy-done | bytes 524312
  1.7 0.0 copy-start.1
  1.7 1.0 %copy-done.1 = f32[1,4,128,256]{3,2,1,0:T(8,128)S(1)} copy-done((f32[1,4,128,256]{3,2,1,0:T(8,128)S(1)}, f32[1,4,128,256]{3,2,1,0:T(8,128)}, u32[]{:S(2)}) %copy-start.1) | copy-done | bytes 524312
  2.7 0.0 copy-start.2
  2.7 1.0 %copy-done.2 = f32[256,512]{1,0:T(8,128)S(1)} copy-done((f32[256,512]{1,0:T(8,128)S(1)}, f32[256,512]{1,0:T(8,128)}, u32[]{:S(2)}) %copy-start.2) | copy-done | bytes 524312
  3.8 0.0 copy-start.3
  3.8 1.0 %copy-done.3 = f32[256,272]{1,0:T(8,128)S(1)} copy-done((f32[256,272]{1,0:T(8,128)S(1)}, f32[256,272]{1,0:T(8,128)}, u32[]{:S(2)}) %copy-start.3) | copy-done | bytes 278552
  4.8 0.0 copy-start.4
  4.8 1.0 %copy-done.4 = f32[272,256]{1,0:T(8,128)S(1)} copy-done((f32[272,256]{1,0:T(8,128)S(1)}, f32[272,256]{1,0:T(8,128)}, u32[]{:S(2)}) %copy-start.4) | copy-done | bytes 278552
  5.7 0.0 copy-start.5
  5.7 0.9 %copy-done.5 = f32[256,256]{1,0:T(8,128)S(1)} copy-done((f32[256,256]{1,0:T(8,128)S(1)}, f32[256,256]{1,0:T(8,128)}, u32[]{:S(2)}) %copy-start.5) | copy-done | bytes 262168
  6.7 0.0 copy-start.6
  6.7 0.9 %copy-done.6 = f32[256,256]{1,0:T(8,128)S(1)} copy-done((f32[256,256]{1,0:T(8,128)S(1)}, f32[256,256]{1,0:T(8,128)}, u32[]{:S(2)}) %copy-start.6) | copy-done | bytes 262168
  7.6 0.0 copy-start.7
  7.6 0.9 %copy-done.7 = f32[256,256]{1,0:T(8,128)S(1)} copy-done((f32[256,256]{1,0:T(8,128)S(1)}, f32[256,256]{1,0:T(8,128)}, u32[]{:S(2)}) %copy-start.7) | copy-done | bytes 262168
  8.6 0.0 copy-start.8
  8.6 0.9 %copy-done.8 = f32[256,256]{1,0:T(8,128)S(1)} copy-done((f32[256,256]{1,0:T(8,128)S(1)}, f32[256,256]{1,0:T(8,128)}, u32[]{:S(2)}) %copy-start.8) | copy-done | bytes 262168
  9.5 0.0 copy-start.9
  9.5 0.9 %copy-done.9 = f32[256,256]{1,0:T(8,128)S(1)} copy-done((f32[256,256]{1,0:T(8,128)S(1)}, f32[256,256]{1,0:T(8,128)}, u32[]{:S(2)}) %copy-start.9) | copy-done | bytes 262168
  10.5 0.0 copy-start.10
  10.5 0.9 %copy-done.10 = f32[256,256]{1,0:T(8,128)S(1)} copy-done((f32[256,256]{1,0:T(8,128)S(1)}, f32[256,256]{1,0:T(8,128)}, u32[]{:S(2)}) %copy-start.10) | copy-done | bytes 262168
  11.4 0.0 copy-start.11
  11.4 0.9 %copy-done.11 = f32[256,256]{1,0:T(8,128)S(1)} copy-done((f32[256,256]{1,0:T(8,128)S(1)}, f32[256,256]{1,0:T(8,128)}, u32[]{:S(2)}) %copy-start.11) | copy-done | bytes 262168
  12.4 0.0 copy-start.12
  12.4 0.9 %copy-done.12 = f32[256,256]{1,0:T(8,128)S(1)} copy-done((f32[256,256]{1,0:T(8,128)S(1)}, f32[256,256]{1,0:T(8,128)}, u32[]{:S(2)}) %copy-start.12) | copy-done | bytes 262168
  13.3 0.0 copy-start.13
  13.3 0.9 %copy-done.13 = f32[256,136]{1,0:T(8,128)S(1)} copy-done((f32[256,136]{1,0:T(8,128)S(1)}, f32[256,136]{1,0:T(8,128)}, u32[]{:S(2)}) %copy-start.13) | copy-done | bytes 139288
  14.3 0.0 copy-start.14
  14.3 0.9 %copy-done.14 = f32[256,256]{1,0:T(8,128)S(1)} copy-done((f32[256,256]{1,0:T(8,128)S(1)}, f32[256,256]{1,0:T(8,128)}, u32[]{:S(2)}) %copy-start.14) | copy-done | bytes 262168
  15.2 0.0 copy-start.15
  15.2 0.9 %copy-done.15 = f32[136,256]{1,0:T(8,128)S(1)} copy-done((f32[136,256]{1,0:T(8,128)S(1)}, f32[136,256]{1,0:T(8,128)}, u32[]{:S(2)}) %copy-start.15) | copy-done | bytes 139288
  16.1 0.0 copy-start.16
  16.1 0.9 %copy-done.16 = f32[128,256]{1,0:T(8,128)S(1)} copy-done((f32[128,256]{1,0:T(8,128)S(1)}, f32[128,256]{1,0:T(8,128)}, u32[]{:S(2)}) %copy-start.16) | copy-done | bytes 131096
  17.0 0.0 copy-start.17
  17.0 0.9 %copy-done.17 = f32[256,128]{1,0:T(8,128)S(1)} copy-done((f32[256,128]{1,0:T(8,128)S(1)}, f32[256,128]{1,0:T(8,128)}, u32[]{:S(2)}) %copy-start.17) | copy-done | bytes 131096
  17.9 0.0 copy-start.18
  17.9 0.8 %copy-done.18 = f32[1,128,128]{2,1,0:T(8,128)S(1)} copy-done((f32[1,128,128]{2,1,0:T(8,128)S(1)}, f32[1,128,128]{2,1,0:T(8,128)}, u32[]{:S(2)}) %copy-start.18) | copy-done | bytes 65560
  18.8 0.0 copy-start.19
  18.8 0.8 %copy-done.19 = f32[1,128,128]{2,1,0:T(8,128)S(1)} copy-done((f32[1,128,128]{2,1,0:T(8,128)S(1)}, f32[1,128,128]{2,1,0:T(8,128)}, u32[]{:S(2)}) %copy-start.19) | copy-done | bytes 65560
  19.6 0.0 copy-start.20
  19.6 0.8 %copy-done.20 = f32[128,128]{1,0:T(8,128)S(1)} copy-done((f32[128,128]{1,0:T(8,128)S(1)}, f32[128,128]{1,0:T(8,128)}, u32[]{:S(2)}) %copy-start.20) | copy-done | bytes 65560
  20.5 50.4 %step.1 = (f32[4,128,256]{2,1,0:T(8,128)S(1)}, f32[128,128]{1,0:T(8,128)S(1)}) custom-call(f32[4,128,256]{2,1,0:T(8,128)S(1)} %bitcast.6, f32[4,128,256]{2,1,0:T(8,128)S(1)} %bitcast.7, f32[128,128]{1,0:T(8,128)S(1)} %bitcast.9, f32[128,128]{1,0:T(8,128)S(1)} %bitcast.10, f32[256,256]{1,0:T(8,128)S(1)} %copy-done.14, f32[256,128]{1,0:T(8,128)S(1)} %copy-done.17, ...), custom_call_target="tpu_custom_call" | custom-call | tf_op jit(solution)/shard_map/step/pallas_call | solution.py:352
  70.8 0.8 %copy.26 = f32[1,4,128,256]{3,2,1,0:T(8,128)} copy(f32[1,4,128,256]{3,2,1,0:T(8,128)S(1)} %bitcast.8) | data formatting | bytes 1048576
  71.6 0.6 copy.27
Async XLA Ops:
  0.6 1.0 %copy-start = (f32[1,4,128,256]{3,2,1,0:T(8,128)S(1)}, f32[1,4,128,256]{3,2,1,0:T(8,128)}, u32[]{:S(2)}) copy-start(f32[1,4,128,256]{3,2,1,0:T(8,128)} %param.22) | copy-start | bytes 1572868
  1.7 1.0 %copy-start.1 = (f32[1,4,128,256]{3,2,1,0:T(8,128)S(1)}, f32[1,4,128,256]{3,2,1,0:T(8,128)}, u32[]{:S(2)}) copy-start(f32[1,4,128,256]{3,2,1,0:T(8,128)} %param.23) | copy-start | bytes 1572868
  2.7 1.0 %copy-start.2 = (f32[256,512]{1,0:T(8,128)S(1)}, f32[256,512]{1,0:T(8,128)}, u32[]{:S(2)}) copy-start(f32[256,512]{1,0:T(8,128)} %constant.51.clone.refs_19_) | copy-start | bytes 1572868
  3.8 1.0 %copy-start.3 = (f32[256,272]{1,0:T(8,128)S(1)}, f32[256,272]{1,0:T(8,128)}, u32[]{:S(2)}) copy-start(f32[256,272]{1,0:T(8,128)} %constant.50.clone.refs_18_) | copy-start | bytes 835588
  4.8 1.0 %copy-start.4 = (f32[272,256]{1,0:T(8,128)S(1)}, f32[272,256]{1,0:T(8,128)}, u32[]{:S(2)}) copy-start(f32[272,256]{1,0:T(8,128)} %constant.49.clone.refs_17_) | copy-start | bytes 835588
  5.7 0.9 %copy-start.5 = (f32[256,256]{1,0:T(8,128)S(1)}, f32[256,256]{1,0:T(8,128)}, u32[]{:S(2)}) copy-start(f32[256,256]{1,0:T(8,128)} %constant.48.clone.refs_16_) | copy-start | bytes 786436
  6.7 0.9 %copy-start.6 = (f32[256,256]{1,0:T(8,128)S(1)}, f32[256,256]{1,0:T(8,128)}, u32[]{:S(2)}) copy-start(f32[256,256]{1,0:T(8,128)} %constant.47.clone.refs_15_) | copy-start | bytes 786436
  7.6 0.9 %copy-start.7 = (f32[256,256]{1,0:T(8,128)S(1)}, f32[256,256]{1,0:T(8,128)}, u32[]{:S(2)}) copy-start(f32[256,256]{1,0:T(8,128)} %constant.46.clone.refs_14_) | copy-start | bytes 786436
  8.6 0.9 %copy-start.8 = (f32[256,256]{1,0:T(8,128)S(1)}, f32[256,256]{1,0:T(8,128)}, u32[]{:S(2)}) copy-start(f32[256,256]{1,0:T(8,128)} %constant.45.clone.refs_13_) | copy-start | bytes 786436
  9.5 0.9 %copy-start.9 = (f32[256,256]{1,0:T(8,128)S(1)}, f32[256,256]{1,0:T(8,128)}, u32[]{:S(2)}) copy-start(f32[256,256]{1,0:T(8,128)} %constant.44.clone.refs_12_) | copy-start | bytes 786436
  10.5 0.9 %copy-start.10 = (f32[256,256]{1,0:T(8,128)S(1)}, f32[256,256]{1,0:T(8,128)}, u32[]{:S(2)}) copy-start(f32[256,256]{1,0:T(8,128)} %constant.43.clone.refs_11_) | copy-start | bytes 786436
  11.4 0.9 %copy-start.11 = (f32[256,256]{1,0:T(8,128)S(1)}, f32[256,256]{1,0:T(8,128)}, u32[]{:S(2)}) copy-start(f32[256,256]{1,0:T(8,128)} %constant.42.clone.refs_10_) | copy-start | bytes 786436
  12.4 0.9 %copy-start.12 = (f32[256,256]{1,0:T(8,128)S(1)}, f32[256,256]{1,0:T(8,128)}, u32[]{:S(2)}) copy-start(f32[256,256]{1,0:T(8,128)} %constant.41.clone.refs_9_) | copy-start | bytes 786436
  13.3 0.9 %copy-start.13 = (f32[256,136]{1,0:T(8,128)S(1)}, f32[256,136]{1,0:T(8,128)}, u32[]{:S(2)}) copy-start(f32[256,136]{1,0:T(8,128)} %constant.39.clone.refs_7_) | copy-start | bytes 417796
  14.3 0.9 %copy-start.14 = (f32[256,256]{1,0:T(8,128)S(1)}, f32[256,256]{1,0:T(8,128)}, u32[]{:S(2)}) copy-start(f32[256,256]{1,0:T(8,128)} %constant.36.clone.refs_4_) | copy-start | bytes 786436
  15.2 0.9 %copy-start.15 = (f32[136,256]{1,0:T(8,128)S(1)}, f32[136,256]{1,0:T(8,128)}, u32[]{:S(2)}) copy-start(f32[136,256]{1,0:T(8,128)} %constant.40.clone.refs_8_) | copy-start | bytes 417796
  16.1 0.9 %copy-start.16 = (f32[128,256]{1,0:T(8,128)S(1)}, f32[128,256]{1,0:T(8,128)}, u32[]{:S(2)}) copy-start(f32[128,256]{1,0:T(8,128)} %constant.38.clone.refs_6_) | copy-start | bytes 393220
  17.0 0.9 %copy-start.17 = (f32[256,128]{1,0:T(8,128)S(1)}, f32[256,128]{1,0:T(8,128)}, u32[]{:S(2)}) copy-start(f32[256,128]{1,0:T(8,128)} %constant.37.clone.refs_5_) | copy-start | bytes 393220
  17.9 0.8 %copy-start.18 = (f32[1,128,128]{2,1,0:T(8,128)S(1)}, f32[1,128,128]{2,1,0:T(8,128)}, u32[]{:S(2)}) copy-start(f32[1,128,128]{2,1,0:T(8,128)} %param.24) | copy-start | bytes 196612
  18.8 0.8 %copy-start.19 = (f32[1,128,128]{2,1,0:T(8,128)S(1)}, f32[1,128,128]{2,1,0:T(8,128)}, u32[]{:S(2)}) copy-start(f32[1,128,128]{2,1,0:T(8,128)} %param.25) | copy-start | bytes 196612
  19.6 0.8 %copy-start.20 = (f32[128,128]{1,0:T(8,128)S(1)}, f32[128,128]{1,0:T(8,128)}, u32[]{:S(2)}) copy-start(f32[128,128]{1,0:T(8,128)} %constant.53.clone.refs_21_) | copy-start | bytes 196612
where the time goes:
time: 73.1 us; the launch traced here: 72.2 us
  Pallas kernels  50.4 us (69%)
  local copies, waits for them, and re-layouts  21.2 us (29%)
    pallas_call x1, Pallas kernels, on_device(): pl.pallas_call(body, out_shape=(jax.ShapeDtypeStruct((planes, rows, cols)...  50.4 us
    unnamed x44, local copies, waits for them, and re-layouts  21.2 us

commit v1 on v0

--- a/solution.py
+++ b/solution.py
@@ -159,13 +159,15 @@
 
 
 def kernel(tiles, depths, planes, rows, cols, *refs):
-    obj, obs, phase_ref, amp_ref = refs[:4]
-    t = dict(zip(NAMES, refs[4 : 4 + len(NAMES)]))
-    out_obj, out_phase = refs[4 + len(NAMES) : 6 + len(NAMES)]
+    count = len(NAMES)
+    obj_in, obs_in, phase_in, amp_in = refs[:4]
+    table_in = refs[4 : 4 + count]
+    out_obj, out_phase = refs[4 + count : 6 + count]
+    t = dict(zip(NAMES, refs[6 + count : 6 + 2 * count]))
     (
-        strip, rstrip, work_e, work_o, spec_e, spec_o, share, part, mine, full, sums,
+        obs, phase_ref, amp_ref, load_sem, strip, rstrip, work_e, work_o, spec_e, spec_o, share, part, mine, full, sums,
         h1s, h1r, h2s, h2r, s1, r1, s2, r2, s3, r3,
-    ) = refs[6 + len(NAMES) :]
+    ) = refs[6 + 2 * count :]
     me = lax.axis_index("tile")
     layer = lax.axis_index("depth")
     span = rows + 2 * HALF
@@ -175,7 +177,22 @@
         pl.semaphore_signal(barrier, 1, device_id={"tile": lax.rem(me + off, tiles)}, device_id_type=MESH)
     for off in range(1, depths):
         pl.semaphore_signal(barrier, 1, device_id={"depth": lax.rem(layer + off, depths)}, device_id_type=MESH)
-    pl.semaphore_wait(barrier, tiles + depths - 2)
+
+    loads = {"phase": pltpu.make_async_copy(phase_in, phase_ref, load_sem.at[0])}
+    loads["amp"] = pltpu.make_async_copy(amp_in, amp_ref, load_sem.at[1])
+    loads["obj"] = pltpu.make_async_copy(obj_in, strip.at[:, pl.ds(HALF, rows)], load_sem.at[2])
+    loads["obs"] = pltpu.make_async_copy(obs_in, obs, load_sem.at[3])
+    for index, name in enumerate(NAMES):
+        loads[name] = pltpu.make_async_copy(table_in[index], t[name], load_sem.at[4 + index])
+    for name in ("phase", "amp", "aperture", "left", "right", "obj"):
+        loads[name].start()
+    for name in loads:
+        if name not in ("phase", "amp", "aperture", "left", "right", "obj"):
+            loads[name].start()
+
+    def ready(*names):
+        for name in names:
+            loads[name].wait()
 
     def halo(source, source_row, buffer, sends, recvs, plane, direction):
         peer = lax.rem(me + (1 if direction == 0 else tiles - 1), tiles)
@@ -188,14 +205,10 @@
         )
 
     def halo1(plane, direction):
-        return halo(obj, 0, strip, h1s, h1r, plane, direction)
+        return halo(strip, HALF, strip, h1s, h1r, plane, direction)
 
     def halo2(plane, direction):
         return halo(rstrip, HALF, rstrip, h2s, h2r, plane, direction)
-
-    for plane in range(planes):
-        halo1(plane, 0).start()
-        halo1(plane, 1).start()
 
     def spread_of(angle):
         sine, cosine = sin_cos(angle)
@@ -229,12 +242,17 @@
             work_o[at] = times(spec_o[at], kernel_o)
         return mm(work_e[...], t["even_back"][...]), mm(work_o[...], t["odd_back"][...])
 
+    ready("phase", "amp", "aperture", "left", "right")
     phase = phase_ref[...]
     field, real, imag, total, psf = spread_of(phase)
+    ready("obj")
+    pl.semaphore_wait(barrier, tiles + depths - 2)
+    for plane in range(planes):
+        halo1(plane, 0).start()
+        halo1(plane, 1).start()
+    ready(*[name for name in loads if name not in ("phase", "amp", "aperture", "left", "right", "obj")])
     kernel_e, kernel_o = spectrum_of(psf)
 
-    for plane in range(planes):
-        strip[plane, pl.ds(HALF, rows)] = obj[plane]
     for plane in range(planes):
         halo1(plane, 0).wait()
         halo1(plane, 1).wait()
@@ -335,7 +353,7 @@
     even = mm(work_e[...], t["even_back"][...])
     odd = mm(work_o[...], t["odd_back"][...])
     for plane in range(planes):
-        out_obj[plane] = obj[plane] * back(plane, even, odd)
+        out_obj[plane] = strip[plane, pl.ds(HALF, rows)] * back(plane, even, odd)
 
 
 def on_device(objects, observed, pupil_phase, pupil_amplitude):
@@ -355,9 +373,14 @@
             jax.ShapeDtypeStruct((planes, rows, cols), f32),
             jax.ShapeDtypeStruct((PUP, PUP), f32),
         ),
-        in_specs=[pl.BlockSpec(memory_space=vmem)] * (4 + len(NAMES)),
+        in_specs=[pl.BlockSpec(memory_space=pltpu.HBM)] * (4 + len(NAMES)),
         out_specs=(pl.BlockSpec(memory_space=vmem), pl.BlockSpec(memory_space=vmem)),
-        scratch_shapes=[
+        scratch_shapes=[vmem(table[name].shape, f32) for name in NAMES]
+        + [
+            vmem((planes, rows, cols), f32),
+            vmem((PUP, PUP), f32),
+            vmem((PUP, PUP), f32),
+            dma((4 + len(NAMES),)),
             vmem((planes, span, cols), f32),
             vmem((planes, span, cols), f32),
             vmem((planes * half, cols), f32),
@@ -374,7 +397,7 @@
             dma((depths - 1,)), dma((depths - 1,)),
         ],
         compiler_params=pltpu.CompilerParams(
-            collective_id=0, has_side_effects=True, vmem_limit_bytes=48 * 1024 * 1024
+            collective_id=0, has_side_effects=True, vmem_limit_bytes=67043328
         ),
         name="step",
     )(objects[0], observed[0], pupil_phase[0], pupil_amplitude[0], *[table[name] for name in NAMES])

time: 73.1 us -> 53.5 us (0.73)
  local copies, waits for them, and re-layouts: 21.2 us -> 2.53 us
    unnamed x44 -> x4, local copies, waits for them, and re-layouts: 21.2 us -> 2.53 us
where the time goes in v1:
time: 53.5 us; the launch traced here: 53.4 us
  Pallas kernels  50.2 us (94%)
  local copies, waits for them, and re-layouts  2.53 us (5%)
  between operations  0.65 us (1%)
    pallas_call x1, Pallas kernels, on_device(): pl.pallas_call(body, out_shape=(jax.ShapeDtypeStruct((planes, rows, cols)...  50.2 us
    unnamed x4, local copies, waits for them, and re-layouts  2.53 us

profile of v1, /device:TPU:1, one launch (start us, length us, event | category | flops | bytes accessed | tf_op | source)
XLA Modules:
  0.0 53.4 jit_solution(15925549741621895455)
XLA Ops:
  0.6 50.2 %step.1 = (f32[4,128,256]{2,1,0:T(8,128)}, f32[128,128]{1,0:T(8,128)}) custom-call(f32[4,128,256]{2,1,0:T(8,128)} %bitcast.6, f32[4,128,256]{2,1,0:T(8,128)} %bitcast.7, f32[128,128]{1,0:T(8,128)} %bitcast.9, f32[128,128]{1,0:T(8,128)} %bitcast.10, f32[256,256]{1,0:T(8,128)} %constant.36.clone.refs_4_, f32[256,128]{1,0:T(8,128)} %constant.37.clone.refs_5_, ...), custom_call_target="tpu_custom_call" | custom-call | tf_op jit(solution)/shard_map/step/pallas_call | solution.py:370
  50.8 0.0 copy-start
  50.8 1.9 %copy.26 = f32[1,4,128,256]{3,2,1,0:T(8,128)} copy(f32[1,4,128,256]{3,2,1,0:T(8,128)} %bitcast.8) | data formatting | bytes 1048576
  52.7 0.0 copy-done
  52.7 0.6 %copy.27 = f32[1,128,128]{2,1,0:T(8,128)} copy(f32[1,128,128]{2,1,0:T(8,128)S(1)} %bitcast.11) | data formatting | bytes 131072
Async XLA Ops:
  50.8 1.9 %copy-start = (f32[128,128]{1,0:T(8,128)S(1)}, f32[128,128]{1,0:T(8,128)}, u32[]{:S(2)}) copy-start(f32[128,128]{1,0:T(8,128)} %get-tuple-element.5) | copy-start | bytes 196612

commit v2 on v1

v2 whole, which is shorter than its diff:
```python
import math

import jax
import jax.numpy as jnp
import numpy as np
from jax import lax
from jax.experimental import pallas as pl
from jax.experimental.pallas import tpu as pltpu
from jax.sharding import PartitionSpec as P

HALF = 64
KER = 129
PUP = 128
PAD = 136
BACKGROUND = 0.1
STEP_SIZE = 0.3
EPSILON = 1e-06
RING = 8
SIDES = 2
MESH = pl.DeviceIdType.MESH


def real_form(matrix):
    return np.block([[matrix.real, matrix.imag], [-matrix.imag, matrix.real]])


def tables(rows, cols):
    span = rows + 2 * HALF
    half = span // 2
    omega = 2.0 * np.pi * (2.0 * np.arange(half) + 0.5) / span
    turn = np.exp(-1j * omega[:, None] * np.arange(span)[None, :])
    row_all = np.concatenate([turn.real, turn.imag])
    row_mid = row_all[:, HALF : HALF + rows]
    lag = np.exp(-1j * omega[:, None] * (np.arange(PAD) - HALF)[None, :]) * (np.arange(PAD) < KER)
    row_lag = np.concatenate([lag.real, lag.imag])
    part = cols // 2
    where = np.arange(part)
    even = np.exp(-2j * np.pi * where[:, None] * (2 * where)[None, :] / cols)
    odd = np.exp(-2j * np.pi * where[:, None] * (2 * where + 1)[None, :] / cols)
    outs = np.arange(cols)
    ring = np.exp(-2j * np.pi * (((outs - HALF)[:, None] * np.arange(PUP)[None, :]) % KER) / KER)
    ring = ring * (outs < KER)[:, None]
    left = np.concatenate([ring.real[:PAD], ring.imag[:PAD]])
    right = np.concatenate([ring.real.T, ring.imag.T])
    grid = np.arange(PUP) - (PUP - 1) / 2.0
    aperture = (grid[:, None] ** 2 + grid[None, :] ** 2 <= (PUP / 2.0) ** 2).astype(float)
    named = dict(
        row_all=row_all,
        row_mid=row_mid,
        row_back=row_mid.T * (2.0 / span / cols),
        row_lag=row_lag,
        row_lag_back=row_lag.T * (2.0 / span / cols),
        even=real_form(even),
        odd=real_form(odd),
        left=left,
        right=right,
        aperture=aperture,
    )
    return {name: np.ascontiguousarray(value, dtype=np.float32) for name, value in named.items()}


def fine(left, right):
    return jnp.dot(left, right, precision=lax.Precision.HIGHEST, preferred_element_type=jnp.float32)


def mm(left, right):
    return jnp.dot(left, right, precision=lax.Precision.HIGH, preferred_element_type=jnp.float32)


def sin_cos(angle):
    count = jnp.floor(angle * (2.0 / math.pi) + 0.5)
    rest = angle - count * 1.5703125
    rest = rest - count * 4.8375129699707031e-4
    rest = rest - count * 7.549789954891882e-8
    square = rest * rest
    sine = ((-1.9515295891e-4 * square + 8.3321608736e-3) * square - 1.6666654611e-1) * square * rest + rest
    cosine = (
        (2.443315711809948e-5 * square - 1.388731625493765e-3) * square + 4.166664568298827e-2
    ) * square * square - 0.5 * square + 1.0
    quarter = count - 4.0 * jnp.floor(count * 0.25)
    swap = (quarter == 1.0) | (quarter == 3.0)
    sin_out = jnp.where(swap, cosine, sine)
    cos_out = jnp.where(swap, sine, cosine)
    sin_out = jnp.where(quarter >= 2.0, -sin_out, sin_out)
    cos_out = jnp.where((quarter == 1.0) | (quarter == 2.0), -cos_out, cos_out)
    return sin_out, cos_out


def beside(one, two):
    return jnp.concatenate([one, two], axis=1)


def above(one, two):
    return jnp.concatenate([one, two], axis=0)


def split_cols(rowed):
    half = rowed.shape[0] // 2
    part = rowed.shape[1] // 2
    plus = rowed[:, :part] + rowed[:, part:]
    minus = rowed[:, :part] - rowed[:, part:]
    return beside(plus[:half], plus[half:]), beside(minus[:half], minus[half:])


def join_cols(even, odd):
    part = even.shape[1] // 2
    plus = even + odd
    minus = even - odd
    return above(
        beside(plus[:, :part], minus[:, :part]),
        beside(plus[:, part:], minus[:, part:]),
    )


def times(one, two):
    part = one.shape[1] // 2
    ar, ai, br, bi = one[:, :part], one[:, part:], two[:, :part], two[:, part:]
    return beside(ar * br - ai * bi, ar * bi + ai * br)


def times_conj(one, two):
    part = one.shape[1] // 2
    ar, ai, br, bi = one[:, :part], one[:, part:], two[:, :part], two[:, part:]
    return beside(ar * br + ai * bi, ai * br - ar * bi)


NAMES = ("aperture", "left", "right", "row_lag", "row_all", "even", "odd", "row_back", "row_mid", "row_lag_back")
EARLY = ("phase", "amp", "aperture", "left", "right", "obj")


def kernel(tiles, depths, planes, rows, cols, *refs):
    count = len(NAMES)
    obj_in, obs_in, phase_in, amp_in = refs[:4]
    table_in = refs[4 : 4 + count]
    out_obj, out_phase = refs[4 + count : 6 + count]
    t = dict(zip(NAMES, refs[6 + count : 6 + 2 * count]))
    (
        obs, phase_ref, amp_ref, load_sem, even_back, odd_back, strip, rstrip, spec_e, spec_o,
        share, part, mine, stack, full, square, sums,
        h1s, h1r, h2s, h2r, s1, r1, s2, r2, s3, r3, s4, r4, s5,
    ) = refs[6 + 2 * count :]
    me = lax.axis_index("tile")
    layer = lax.axis_index("depth")
    span = rows + 2 * HALF
    half = span // 2
    slabs = tiles // RING
    slab, spot = me // RING, lax.rem(me, RING)
    lanes = depths // SIDES
    side, lane = layer // lanes, lax.rem(layer, lanes)
    lowest, highest = slab == 0, slab == slabs - 1
    near = slabs // 2
    source_slab = jnp.where(slab < near, slabs - 1, 0)

    def at_tile(tile):
        return {"tile": tile, "depth": layer}

    def at_spot(off):
        return at_tile(slab * RING + lax.rem(spot + off, RING))

    def at_slab(off):
        return at_tile(lax.rem(slab + off, slabs) * RING + spot)

    def at_lane(off):
        return {"tile": me, "depth": side * lanes + lax.rem(lane + off, lanes)}

    def across(to_slab, to_lane):
        return {"tile": to_slab * RING + spot, "depth": (SIDES - 1 - side) * lanes + to_lane}

    barrier = pltpu.get_barrier_semaphore()

    def greet(device):
        pl.semaphore_signal(barrier, 1, device_id=device, device_id_type=MESH)

    greet(at_tile(lax.rem(me + 1, tiles)))
    greet(at_tile(lax.rem(me + tiles - 1, tiles)))
    for off in range(1, RING):
        greet(at_spot(off))
    for off in range(1, slabs):
        greet(at_slab(off))
    for off in range(1, lanes):
        greet(at_lane(off))
    for to_lane in range(lanes):
        greet(across(source_slab, to_lane))
    near_sends = jnp.where(lowest | highest, near * lanes, 0)
    greeted = 2 + RING - 1 + slabs - 1 + lanes - 1 + near_sends

    loads = {"phase": pltpu.make_async_copy(phase_in, phase_ref, load_sem.at[0])}
    loads["amp"] = pltpu.make_async_copy(amp_in, amp_ref, load_sem.at[1])
    loads["obj"] = pltpu.make_async_copy(obj_in, strip.at[:, pl.ds(HALF, rows)], load_sem.at[2])
    loads["obs"] = pltpu.make_async_copy(obs_in, obs, load_sem.at[3])
    for index, name in enumerate(NAMES):
        loads[name] = pltpu.make_async_copy(table_in[index], t[name], load_sem.at[4 + index])
    for name in EARLY:
        loads[name].start()
    for name in loads:
        if name not in EARLY:
            loads[name].start()

    def ready(*names):
        for name in names:
            loads[name].wait()

    def halo(buffer, sends, recvs, plane, direction):
        peer = lax.rem(me + (1 if direction == 0 else tiles - 1), tiles)
        start = rows if direction == 0 else HALF
        target = 0 if direction == 0 else HALF + rows
        slot = 2 * plane + direction
        return pltpu.make_async_remote_copy(
            buffer.at[plane, pl.ds(start, HALF)], buffer.at[plane, pl.ds(target, HALF)],
            sends.at[slot], recvs.at[slot], device_id=at_tile(peer), device_id_type=MESH,
        )

    def halo1(plane, direction):
        return halo(strip, h1s, h1r, plane, direction)

    def halo2(plane, direction):
        return halo(rstrip, h2s, h2r, plane, direction)

    def full_left():
        real, imag = t["left"][:PAD], t["left"][PAD:]
        return above(beside(real, -imag), beside(imag, real))

    def full_right():
        real, imag = t["right"][:PUP], t["right"][PUP:]
        return above(beside(real, imag), beside(-imag, real))

    def spread_of(angle):
        sine, cosine = sin_cos(angle)
        weight = amp_ref[...] * t["aperture"][...]
        field = above(weight * cosine, weight * sine)
        lefts = fine(full_left(), field)
        outer = fine(beside(lefts[:PAD], lefts[PAD:]), full_right())
        real, imag = outer[:, :cols], outer[:, cols:]
        intensity = real * real + imag * imag
        total = jnp.sum(intensity)
        return field, real, imag, total, intensity * (1.0 / total)

    part_cols = cols // 2
    column = lax.broadcasted_iota(jnp.int32, (1, part_cols), 1)
    flip = 1.0 - 2.0 * lax.rem(column, 2).astype(jnp.float32)
    flips = beside(flip, flip)
    turn_on = beside(-flip, flip)
    turn_off = beside(flip, -flip)

    def swapped(value):
        return beside(value[:, part_cols:], value[:, :part_cols])

    def spectrum_of(psf):
        even, odd = split_cols(mm(t["row_lag"][...], psf))
        return mm(even, t["even"][...]) * flips, swapped(mm(odd, t["odd"][...])) * turn_on

    def columns(rowed):
        even, odd = split_cols(rowed)
        return mm(even, t["even"][...]), mm(odd, t["odd"][...])

    def back(even, odd):
        return mm(t["row_back"][...], join_cols(mm(even, even_back[...]), mm(odd, odd_back[...])))

    def blurred(plane, kernel_e, kernel_o):
        at = pl.ds(plane * half, half)
        return back(times(spec_e[at], kernel_e), times(spec_o[at], kernel_o))

    ready("phase", "amp", "aperture", "left", "right")
    phase = phase_ref[...]
    field, real, imag, total, psf = spread_of(phase)
    ready("obj")
    pl.semaphore_wait(barrier, greeted)
    for plane in range(planes):
        halo1(plane, 0).start()
        halo1(plane, 1).start()
    ready(*[name for name in loads if name not in EARLY])
    even_back[...] = t["even"][...].T
    odd_back[...] = t["odd"][...].T
    kernel_e, kernel_o = spectrum_of(psf)

    cross_e = jnp.zeros((half, cols), jnp.float32)
    cross_o = jnp.zeros((half, cols), jnp.float32)
    for plane in range(planes):
        halo1(plane, 0).wait()
        halo1(plane, 1).wait()
        even, odd = columns(mm(t["row_all"][...], strip[plane]))
        at = pl.ds(plane * half, half)
        spec_e[at] = even
        spec_o[at] = odd
        misfit = 1.0 - obs[plane] / (blurred(plane, kernel_e, kernel_o) + BACKGROUND)
        mis_e, mis_o = columns(mm(t["row_mid"][...], misfit))
        cross_e = cross_e + times_conj(mis_e, spec_e[at])
        cross_o = cross_o + times_conj(mis_o, spec_o[at])
    lagged = join_cols(fine(cross_e * flips, even_back[...]), fine(swapped(cross_o) * turn_off, odd_back[...]))
    psf_grad = fine(t["row_lag_back"][...], lagged)

    scale = 2.0 / total
    centred = (psf_grad - jnp.sum(psf_grad * psf)) * scale
    rest = jnp.zeros((cols - PAD, cols), jnp.float32)
    right = full_right()
    lefts = fine(right, jnp.concatenate([centred * real, rest, centred * imag, rest], axis=0))
    pupils = lax.dot_general(
        beside(lefts[:PUP], lefts[PUP:]), right, (((1,), (1,)), ((), ())),
        precision=lax.Precision.HIGHEST, preferred_element_type=jnp.float32,
    )
    mygrad = field[:PUP] * pupils[:, PUP:] - field[PUP:] * pupils[:, :PUP]

    chunk = PUP // RING
    for piece in range(RING):
        share[piece] = mygrad[piece * chunk : (piece + 1) * chunk]

    def scatter(off):
        return pltpu.make_async_remote_copy(
            share.at[lax.rem(spot + off, RING)], part.at[off - 1], s1.at[off - 1], r1.at[off - 1],
            device_id=at_spot(off), device_id_type=MESH,
        )

    def exchange(off):
        return pltpu.make_async_remote_copy(
            mine, stack.at[slab], s2.at[off - 1], r2.at[off - 1],
            device_id=at_slab(off), device_id_type=MESH,
        )

    def gather(off):
        return pltpu.make_async_remote_copy(
            full.at[spot], full.at[spot], s3.at[off - 1], r3.at[off - 1],
            device_id=at_spot(off), device_id_type=MESH,
        )

    def lane_sum(off):
        return pltpu.make_async_remote_copy(
            square, sums.at[layer], s4.at[off - 1], r4.at[layer],
            device_id=at_lane(off), device_id_type=MESH,
        )

    def far_sum(step, to_lane):
        return pltpu.make_async_remote_copy(
            square, sums.at[layer], s5.at[step * lanes + to_lane], r4.at[layer],
            device_id=across(jnp.where(lowest, near, 0) + step, to_lane), device_id_type=MESH,
        )

    for off in range(1, RING):
        scatter(off).start()
    for off in range(1, RING):
        scatter(off).wait()
    summed = share[spot]
    for off in range(1, RING):
        summed = summed + part[off - 1]
    mine[...] = summed
    for off in range(1, slabs):
        exchange(off).start()
    stack[slab] = summed
    for off in range(1, slabs):
        exchange(off).wait()
    summed = stack[0]
    for other in range(1, slabs):
        summed = summed + stack[other]
    full[spot] = summed
    for off in range(1, RING):
        gather(off).start()
    for off in range(1, RING):
        gather(off).wait()
    gradient = jnp.concatenate([full[piece] for piece in range(RING)], axis=0)
    square[...] = jnp.broadcast_to(jnp.sum(gradient * gradient), (8, 128))
    for off in range(1, lanes):
        lane_sum(off).start()

    @pl.when(lowest | highest)
    def _():
        for step in range(near):
            for to_lane in range(lanes):
                far_sum(step, to_lane).start()

    sums[layer] = square[...]
    for off in range(1, depths):
        other = lax.rem(layer + off, depths)
        pltpu.make_async_remote_copy(
            sums.at[other], sums.at[other], s4.at[0], r4.at[other], device_id=at_lane(1), device_id_type=MESH
        ).wait_recv()
    for off in range(1, lanes):
        lane_sum(off).wait_send()

    @pl.when(lowest | highest)
    def _():
        for step in range(near):
            for to_lane in range(lanes):
                far_sum(step, to_lane).wait_send()

    squares = sums[0]
    for other in range(1, depths):
        squares = squares + sums[other]
    mean_square = squares[0:1] * (1.0 / (depths * PUP * PUP))
    new_phase = phase - STEP_SIZE * gradient / jnp.sqrt(mean_square + EPSILON)
    out_phase[...] = new_phase

    _, _, _, _, psf = spread_of(new_phase)
    kernel_e, kernel_o = spectrum_of(psf)
    for plane in range(planes):
        rstrip[plane, pl.ds(HALF, rows)] = obs[plane] / (blurred(plane, kernel_e, kernel_o) + BACKGROUND)
        halo2(plane, 0).start()
        halo2(plane, 1).start()
    for plane in range(planes):
        halo2(plane, 0).wait()
        halo2(plane, 1).wait()
        even, odd = columns(mm(t["row_all"][...], rstrip[plane]))
        correction = back(times_conj(even, kernel_e), times_conj(odd, kernel_o))
        out_obj[plane] = strip[plane, pl.ds(HALF, rows)] * correction


def on_device(objects, observed, pupil_phase, pupil_amplitude):
    tiles, depths = lax.axis_size("tile"), lax.axis_size("depth")
    _, planes, rows, cols = objects.shape
    span = rows + 2 * HALF
    half = span // 2
    table = tables(rows, cols)
    f32 = jnp.float32
    vmem = pltpu.VMEM
    dma = pltpu.SemaphoreType.DMA
    chunk = PUP // RING
    slabs = tiles // RING
    lanes = depths // SIDES
    body = lambda *refs: kernel(tiles, depths, planes, rows, cols, *refs)
    new_objects, new_phase = pl.pallas_call(
        body,
        out_shape=(
            jax.ShapeDtypeStruct((planes, rows, cols), f32),
            jax.ShapeDtypeStruct((PUP, PUP), f32),
        ),
        in_specs=[pl.BlockSpec(memory_space=pltpu.HBM)] * (4 + len(NAMES)),
        out_specs=(pl.BlockSpec(memory_space=vmem), pl.BlockSpec(memory_space=vmem)),
        scratch_shapes=[vmem(table[name].shape, f32) for name in NAMES]
        + [
            vmem((planes, rows, cols), f32),
            vmem((PUP, PUP), f32),
            vmem((PUP, PUP), f32),
            dma((4 + len(NAMES),)),
            vmem((cols, cols), f32),
            vmem((cols, cols), f32),
            vmem((planes, span, cols), f32),
            vmem((planes, span, cols), f32),
            vmem((planes * half, cols), f32),
            vmem((planes * half, cols), f32),
            vmem((RING, chunk, PUP), f32),
            vmem((RING - 1, chunk, PUP), f32),
            vmem((chunk, PUP), f32),
            vmem((slabs, chunk, PUP), f32),
            vmem((RING, chunk, PUP), f32),
            vmem((8, 128), f32),
            vmem((depths, 8, 128), f32),
            dma((2 * planes,)), dma((2 * planes,)), dma((2 * planes,)), dma((2 * planes,)),
            dma((RING - 1,)), dma((RING - 1,)), dma((slabs - 1,)), dma((slabs - 1,)),
            dma((RING - 1,)), dma((RING - 1,)), dma((lanes - 1,)), dma((depths,)),
            dma((slabs // 2 * lanes,)),
        ],
        compiler_params=pltpu.CompilerParams(
            collective_id=0, has_side_effects=True, vmem_limit_bytes=67043328
        ),
        name="step",
    )(objects[0], observed[0], pupil_phase[0], pupil_amplitude[0], *[table[name] for name in NAMES])
    return new_objects[None], new_phase[None]


def solution(mesh):
    return jax.shard_map(
        on_device,
        mesh=mesh,
        in_specs=(
            P("depth", None, "tile", None),
            P("depth", None, "tile", None),
            P("depth", None, None),
            P("depth", None, None),
        ),
        out_specs=(P("depth", None, "tile", None), P("depth", None, None)),
        check_vma=False,
    )
```

time: 53.5 us -> 54.3 us (1.015)
  Pallas kernels: 50.2 us -> 51 us
    pallas_call x1, Pallas kernels: 50.2 us -> 51 us  [on_device(): pl.pallas_call(body, out_shape=(jax.ShapeDtypeStruct((planes, rows, cols)...]
where the time goes in v2:
time: 54.3 us; the launch traced here: 54.2 us
  Pallas kernels  51 us (94%)
  local copies, waits for them, and re-layouts  2.53 us (5%)
  between operations  0.65 us (1%)
    pallas_call x1, Pallas kernels, on_device(): pl.pallas_call(body, out_shape=(jax.ShapeDtypeStruct((planes, rows, cols)...  51 us
    unnamed x4, local copies, waits for them, and re-layouts  2.53 us

profile of v2, /device:TPU:1, one launch (start us, length us, event | category | flops | bytes accessed | tf_op | source)
XLA Modules:
  0.0 54.2 jit_solution(209729490861549694)
XLA Ops:
  0.6 51.0 %step.1 = (f32[4,128,256]{2,1,0:T(8,128)}, f32[128,128]{1,0:T(8,128)}) custom-call(f32[4,128,256]{2,1,0:T(8,128)} %bitcast.7, f32[4,128,256]{2,1,0:T(8,128)} %bitcast.8, f32[128,128]{1,0:T(8,128)} %bitcast.9, f32[128,128]{1,0:T(8,128)} %bitcast.10, f32[128,128]{1,0:T(8,128)} %constant.20.clone.refs_4_, f32[272,128]{1,0:T(8,128)} %constant.21.clone.refs_5_, ...), custom_call_target="tpu_custom_call" | custom-call | tf_op jit(solution)/shard_map/step/pallas_call | solution.py:418
  51.6 0.0 copy-start
  51.6 1.9 %copy.18 = f32[1,4,128,256]{3,2,1,0:T(8,128)} copy(f32[1,4,128,256]{3,2,1,0:T(8,128)} %bitcast.6) | data formatting | bytes 1048576
  53.5 0.0 copy-done
  53.5 0.6 %copy.19 = f32[1,128,128]{2,1,0:T(8,128)} copy(f32[1,128,128]{2,1,0:T(8,128)S(1)} %bitcast.11) | data formatting | bytes 131072
Async XLA Ops:
  51.6 1.9 %copy-start = (f32[128,128]{1,0:T(8,128)S(1)}, f32[128,128]{1,0:T(8,128)}, u32[]{:S(2)}) copy-start(f32[128,128]{1,0:T(8,128)} %get-tuple-element.5) | copy-start | bytes 196612

commit v3 on v2

--- a/solution.py
+++ b/solution.py
@@ -17,6 +17,7 @@
 EPSILON = 1e-06
 RING = 8
 SIDES = 2
+GROUP = 2
 MESH = pl.DeviceIdType.MESH
 
 
@@ -59,10 +60,6 @@
     return {name: np.ascontiguousarray(value, dtype=np.float32) for name, value in named.items()}
 
 
-def fine(left, right):
-    return jnp.dot(left, right, precision=lax.Precision.HIGHEST, preferred_element_type=jnp.float32)
-
-
 def mm(left, right):
     return jnp.dot(left, right, precision=lax.Precision.HIGH, preferred_element_type=jnp.float32)
 
@@ -110,6 +107,17 @@
         beside(plus[:, :part], minus[:, :part]),
         beside(plus[:, part:], minus[:, part:]),
     )
+
+
+def stacked(values):
+    return values[0] if len(values) == 1 else jnp.concatenate(values, axis=0)
+
+
+def summed_over(value, rows):
+    total = value[:rows]
+    for at in range(rows, value.shape[0], rows):
+        total = total + value[at : at + rows]
+    return total
 
 
 def times(one, two):
@@ -228,12 +236,12 @@
         sine, cosine = sin_cos(angle)
         weight = amp_ref[...] * t["aperture"][...]
         field = above(weight * cosine, weight * sine)
-        lefts = fine(full_left(), field)
-        outer = fine(beside(lefts[:PAD], lefts[PAD:]), full_right())
+        lefts = mm(full_left(), field)
+        outer = mm(beside(lefts[:PAD], lefts[PAD:]), full_right())
         real, imag = outer[:, :cols], outer[:, cols:]
         intensity = real * real + imag * imag
         total = jnp.sum(intensity)
-        return field, real, imag, total, intensity * (1.0 / total)
+        return field, real, imag, total, intensity
 
     part_cols = cols // 2
     column = lax.broadcasted_iota(jnp.int32, (1, part_cols), 1)
@@ -245,24 +253,45 @@
     def swapped(value):
         return beside(value[:, part_cols:], value[:, :part_cols])
 
-    def spectrum_of(psf):
-        even, odd = split_cols(mm(t["row_lag"][...], psf))
-        return mm(even, t["even"][...]) * flips, swapped(mm(odd, t["odd"][...])) * turn_on
+    def spectrum_of(intensity, total):
+        even, odd = split_cols(mm(t["row_lag"][...], intensity))
+        share_of = 1.0 / total
+        return (
+            mm(even, t["even"][...]) * (flips * share_of),
+            swapped(mm(odd, t["odd"][...])) * (turn_on * share_of),
+        )
 
     def columns(rowed):
-        even, odd = split_cols(rowed)
-        return mm(even, t["even"][...]), mm(odd, t["odd"][...])
+        pairs = [split_cols(value) for value in rowed]
+        return (
+            mm(stacked([even for even, _ in pairs]), t["even"][...]),
+            mm(stacked([odd for _, odd in pairs]), t["odd"][...]),
+        )
 
     def back(even, odd):
-        return mm(t["row_back"][...], join_cols(mm(even, even_back[...]), mm(odd, odd_back[...])))
-
-    def blurred(plane, kernel_e, kernel_o):
-        at = pl.ds(plane * half, half)
-        return back(times(spec_e[at], kernel_e), times(spec_o[at], kernel_o))
+        even, odd = mm(even, even_back[...]), mm(odd, odd_back[...])
+        return [
+            mm(t["row_back"][...], join_cols(even[at : at + half], odd[at : at + half]))
+            for at in range(0, even.shape[0], half)
+        ]
+
+    def twice(value):
+        return stacked([value] * GROUP)
+
+    def blurred(first, kernel_e, kernel_o):
+        at = pl.ds(first * half, GROUP * half)
+        return back(times(spec_e[at], twice(kernel_e)), times(spec_o[at], twice(kernel_o)))
+
+    groups = range(0, planes, GROUP)
+
+    def wait_group(halo_of, first):
+        for plane in range(first, first + GROUP):
+            halo_of(plane, 0).wait()
+            halo_of(plane, 1).wait()
 
     ready("phase", "amp", "aperture", "left", "right")
     phase = phase_ref[...]
-    field, real, imag, total, psf = spread_of(phase)
+    field, real, imag, total, intensity = spread_of(phase)
     ready("obj")
     pl.semaphore_wait(barrier, greeted)
     for plane in range(planes):
@@ -271,32 +300,33 @@
     ready(*[name for name in loads if name not in EARLY])
     even_back[...] = t["even"][...].T
     odd_back[...] = t["odd"][...].T
-    kernel_e, kernel_o = spectrum_of(psf)
+    kernel_e, kernel_o = spectrum_of(intensity, total)
 
     cross_e = jnp.zeros((half, cols), jnp.float32)
     cross_o = jnp.zeros((half, cols), jnp.float32)
-    for plane in range(planes):
-        halo1(plane, 0).wait()
-        halo1(plane, 1).wait()
-        even, odd = columns(mm(t["row_all"][...], strip[plane]))
-        at = pl.ds(plane * half, half)
+    for first in groups:
+        wait_group(halo1, first)
+        mates = range(first, first + GROUP)
+        even, odd = columns([mm(t["row_all"][...], strip[plane]) for plane in mates])
+        at = pl.ds(first * half, GROUP * half)
         spec_e[at] = even
         spec_o[at] = odd
-        misfit = 1.0 - obs[plane] / (blurred(plane, kernel_e, kernel_o) + BACKGROUND)
-        mis_e, mis_o = columns(mm(t["row_mid"][...], misfit))
-        cross_e = cross_e + times_conj(mis_e, spec_e[at])
-        cross_o = cross_o + times_conj(mis_o, spec_o[at])
-    lagged = join_cols(fine(cross_e * flips, even_back[...]), fine(swapped(cross_o) * turn_off, odd_back[...]))
-    psf_grad = fine(t["row_lag_back"][...], lagged)
+        blurs = back(times(even, twice(kernel_e)), times(odd, twice(kernel_o)))
+        misfits = [1.0 - obs[plane] / (blur + BACKGROUND) for plane, blur in zip(mates, blurs)]
+        mis_e, mis_o = columns([mm(t["row_mid"][...], misfit) for misfit in misfits])
+        cross_e = cross_e + summed_over(times_conj(mis_e, spec_e[at]), half)
+        cross_o = cross_o + summed_over(times_conj(mis_o, spec_o[at]), half)
+    lagged = join_cols(mm(cross_e * flips, even_back[...]), mm(swapped(cross_o) * turn_off, odd_back[...]))
+    psf_grad = mm(t["row_lag_back"][...], lagged)
 
     scale = 2.0 / total
-    centred = (psf_grad - jnp.sum(psf_grad * psf)) * scale
+    centred = (psf_grad - jnp.sum(psf_grad * intensity) / total) * scale
     rest = jnp.zeros((cols - PAD, cols), jnp.float32)
     right = full_right()
-    lefts = fine(right, jnp.concatenate([centred * real, rest, centred * imag, rest], axis=0))
+    lefts = mm(right, jnp.concatenate([centred * real, rest, centred * imag, rest], axis=0))
     pupils = lax.dot_general(
         beside(lefts[:PUP], lefts[PUP:]), right, (((1,), (1,)), ((), ())),
-        precision=lax.Precision.HIGHEST, preferred_element_type=jnp.float32,
+        precision=lax.Precision.HIGH, preferred_element_type=jnp.float32,
     )
     mygrad = field[:PUP] * pupils[:, PUP:] - field[PUP:] * pupils[:, :PUP]
 
@@ -388,18 +418,29 @@
     new_phase = phase - STEP_SIZE * gradient / jnp.sqrt(mean_square + EPSILON)
     out_phase[...] = new_phase
 
-    _, _, _, _, psf = spread_of(new_phase)
-    kernel_e, kernel_o = spectrum_of(psf)
-    for plane in range(planes):
-        rstrip[plane, pl.ds(HALF, rows)] = obs[plane] / (blurred(plane, kernel_e, kernel_o) + BACKGROUND)
-        halo2(plane, 0).start()
-        halo2(plane, 1).start()
-    for plane in range(planes):
-        halo2(plane, 0).wait()
-        halo2(plane, 1).wait()
-        even, odd = columns(mm(t["row_all"][...], rstrip[plane]))
-        correction = back(times_conj(even, kernel_e), times_conj(odd, kernel_o))
-        out_obj[plane] = strip[plane, pl.ds(HALF, rows)] * correction
+    _, _, _, total, intensity = spread_of(new_phase)
+    kernel_e, kernel_o = spectrum_of(intensity, total)
+    for first in groups:
+        for plane, blur in zip(range(first, first + GROUP), blurred(first, kernel_e, kernel_o)):
+            rstrip[plane, pl.ds(HALF, rows)] = obs[plane] / (blur + BACKGROUND)
+            halo2(plane, 0).start()
+            halo2(plane, 1).start()
+    for first in groups:
+        wait_group(halo2, first)
+        mates = range(first, first + GROUP)
+        even, odd = columns([mm(t["row_all"][...], rstrip[plane]) for plane in mates])
+        corrections = back(times_conj(even, twice(kernel_e)), times_conj(odd, twice(kernel_o)))
+        for plane, correction in zip(mates, corrections):
+            out_obj[plane] = strip[plane, pl.ds(HALF, rows)] * correction
+
+
+def write_kernel(objects, phase, objects_out, phase_out, sem):
+    one = pltpu.make_async_copy(objects, objects_out, sem.at[0])
+    two = pltpu.make_async_copy(phase, phase_out, sem.at[1])
+    one.start()
+    two.start()
+    one.wait()
+    two.wait()
 
 
 def on_device(objects, observed, pupil_phase, pupil_amplitude):
@@ -448,10 +489,24 @@
             dma((slabs // 2 * lanes,)),
         ],
         compiler_params=pltpu.CompilerParams(
-            collective_id=0, has_side_effects=True, vmem_limit_bytes=67043328
+            collective_id=0, has_side_effects=True, vmem_limit_bytes=48 * 1024 * 1024
         ),
         name="step",
-    )(objects[0], observed[0], pupil_phase[0], pupil_amplitude[0], *[table[name] for name in NAMES])
+    )(*[
+        pltpu.with_memory_space_constraint(value, pltpu.HBM)
+        for value in (objects[0], observed[0], pupil_phase[0], pupil_amplitude[0], *[table[name] for name in NAMES])
+    ])
+    new_objects, new_phase = pl.pallas_call(
+        write_kernel,
+        out_shape=(
+            jax.ShapeDtypeStruct((planes, rows, cols), f32),
+            jax.ShapeDtypeStruct((PUP, PUP), f32),
+        ),
+        in_specs=[pl.BlockSpec(memory_space=pl.ANY)] * 2,
+        out_specs=(pl.BlockSpec(memory_space=pltpu.HBM), pl.BlockSpec(memory_space=pltpu.HBM)),
+        scratch_shapes=[dma((2,))],
+        name="write",
+    )(*[pltpu.with_memory_space_constraint(value, vmem) for value in (new_objects, new_phase)])
     return new_objects[None], new_phase[None]
 
 

time: 54.3 us -> 46.3 us (0.85)
  Pallas kernels: 51 us -> 45.5 us
  local copies, waits for them, and re-layouts: 2.53 us -> 0 us
    pallas_call x1, Pallas kernels: 51 us -> 44.7 us  [on_device(): pl.pallas_call(body, out_shape=(jax.ShapeDtypeStruct((planes, rows, cols)...]
    unnamed x4 -> x0, local copies, waits for them, and re-layouts: 2.53 us -> none
    pallas_call x0 -> x1, Pallas kernels: none -> 0.82 us  [on_device(): pl.pallas_call(write_kernel, out_shape=(jax.ShapeDtypeStruct((planes, row...]
where the time goes in v3:
time: 46.3 us; the launch traced here: 46.2 us
  Pallas kernels  45.5 us (98%)
  between operations  0.64 us (1%)
    pallas_call x1, Pallas kernels, on_device(): pl.pallas_call(body, out_shape=(jax.ShapeDtypeStruct((planes, rows, cols)...  44.7 us

profile of v3, /device:TPU:1, one launch (start us, length us, event | category | flops | bytes accessed | tf_op | source)
XLA Modules:
  0.0 46.2 jit_solution(6803456144670383197)
XLA Ops:
  0.6 44.7 %step.1 = (f32[4,128,256]{2,1,0:T(8,128)S(1)}, f32[128,128]{1,0:T(8,128)S(1)}) custom-call(f32[4,128,256]{2,1,0:T(8,128)} %bitcast.6, f32[4,128,256]{2,1,0:T(8,128)} %bitcast.7, f32[128,128]{1,0:T(8,128)} %bitcast.8, f32[128,128]{1,0:T(8,128)} %bitcast.9, f32[128,128]{1,0:T(8,128)} %constant.20.clone.refs_4_, f32[272,128]{1,0:T(8,128)} %constant.21.clone.refs_5_, ...), custom_call_target="tpu_custom_call" | custom-call | tf_op jit(solution)/shard_map/step/pallas_call | solution.py:459
  45.4 0.8 %write.1 = (f32[4,128,256]{2,1,0:T(8,128)}, f32[128,128]{1,0:T(8,128)}) custom-call(f32[4,128,256]{2,1,0:T(8,128)S(1)} %get-tuple-element.6.objects, f32[128,128]{1,0:T(8,128)S(1)} %get-tuple-element.7.phase), custom_call_target="tpu_custom_call" | custom-call | tf_op jit(solution)/shard_map/write/pallas_call | solution.py:499

commit v4 on v3

--- a/solution.py
+++ b/solution.py
@@ -143,9 +143,9 @@
     out_obj, out_phase = refs[4 + count : 6 + count]
     t = dict(zip(NAMES, refs[6 + count : 6 + 2 * count]))
     (
-        obs, phase_ref, amp_ref, load_sem, even_back, odd_back, strip, rstrip, spec_e, spec_o,
-        share, part, mine, stack, full, square, sums,
-        h1s, h1r, h2s, h2r, s1, r1, s2, r2, s3, r3, s4, r4, s5,
+        phase_ref, amp_ref, load_sem, even_back, odd_back, big, obs, spec_e, spec_o,
+        share, part, mine, stack, full, square, sums, spots, spot_sum,
+        h1s, h1r, h2s, h2r, h3s, h3r, s1, r1, s2, r2, s3, r3, s4, r4, s5, s6, r6,
     ) = refs[6 + 2 * count :]
     me = lax.axis_index("tile")
     layer = lax.axis_index("depth")
@@ -194,8 +194,8 @@
 
     loads = {"phase": pltpu.make_async_copy(phase_in, phase_ref, load_sem.at[0])}
     loads["amp"] = pltpu.make_async_copy(amp_in, amp_ref, load_sem.at[1])
-    loads["obj"] = pltpu.make_async_copy(obj_in, strip.at[:, pl.ds(HALF, rows)], load_sem.at[2])
-    loads["obs"] = pltpu.make_async_copy(obs_in, obs, load_sem.at[3])
+    loads["obj"] = pltpu.make_async_copy(obj_in, big.at[:, pl.ds(rows, rows)], load_sem.at[2])
+    loads["obs"] = pltpu.make_async_copy(obs_in, obs.at[:, pl.ds(HALF, rows)], load_sem.at[3])
     for index, name in enumerate(NAMES):
         loads[name] = pltpu.make_async_copy(table_in[index], t[name], load_sem.at[4 + index])
     for name in EARLY:
@@ -208,21 +208,22 @@
         for name in names:
             loads[name].wait()
 
-    def halo(buffer, sends, recvs, plane, direction):
+    def halo(buffer, first, mine_from, theirs_to, sends, recvs, plane, direction):
         peer = lax.rem(me + (1 if direction == 0 else tiles - 1), tiles)
-        start = rows if direction == 0 else HALF
-        target = 0 if direction == 0 else HALF + rows
         slot = 2 * plane + direction
         return pltpu.make_async_remote_copy(
-            buffer.at[plane, pl.ds(start, HALF)], buffer.at[plane, pl.ds(target, HALF)],
+            buffer.at[plane, pl.ds(first + mine_from, HALF)], buffer.at[plane, pl.ds(first + theirs_to, HALF)],
             sends.at[slot], recvs.at[slot], device_id=at_tile(peer), device_id_type=MESH,
         )
 
     def halo1(plane, direction):
-        return halo(strip, h1s, h1r, plane, direction)
+        return halo(big, rows, *((rows - HALF, -HALF) if direction == 0 else (0, rows)), h1s, h1r, plane, direction)
 
     def halo2(plane, direction):
-        return halo(rstrip, h2s, h2r, plane, direction)
+        return halo(big, rows, *((0, -rows) if direction == 0 else (HALF, rows + HALF)), h2s, h2r, plane, direction)
+
+    def halo3(plane, direction):
+        return halo(obs, HALF, *((rows - HALF, -HALF) if direction == 0 else (0, rows)), h3s, h3r, plane, direction)
 
     def full_left():
         real, imag = t["left"][:PAD], t["left"][PAD:]
@@ -278,10 +279,6 @@
     def twice(value):
         return stacked([value] * GROUP)
 
-    def blurred(first, kernel_e, kernel_o):
-        at = pl.ds(first * half, GROUP * half)
-        return back(times(spec_e[at], twice(kernel_e)), times(spec_o[at], twice(kernel_o)))
-
     groups = range(0, planes, GROUP)
 
     def wait_group(halo_of, first):
@@ -297,7 +294,13 @@
     for plane in range(planes):
         halo1(plane, 0).start()
         halo1(plane, 1).start()
+    for plane in range(planes):
+        halo2(plane, 0).start()
+        halo2(plane, 1).start()
     ready(*[name for name in loads if name not in EARLY])
+    for plane in range(planes):
+        halo3(plane, 0).start()
+        halo3(plane, 1).start()
     even_back[...] = t["even"][...].T
     odd_back[...] = t["odd"][...].T
     kernel_e, kernel_o = spectrum_of(intensity, total)
@@ -307,15 +310,12 @@
     for first in groups:
         wait_group(halo1, first)
         mates = range(first, first + GROUP)
-        even, odd = columns([mm(t["row_all"][...], strip[plane]) for plane in mates])
-        at = pl.ds(first * half, GROUP * half)
-        spec_e[at] = even
-        spec_o[at] = odd
+        even, odd = columns([mm(t["row_all"][...], big[plane, pl.ds(HALF, span)]) for plane in mates])
         blurs = back(times(even, twice(kernel_e)), times(odd, twice(kernel_o)))
-        misfits = [1.0 - obs[plane] / (blur + BACKGROUND) for plane, blur in zip(mates, blurs)]
+        misfits = [1.0 - obs[plane, pl.ds(HALF, rows)] / (blur + BACKGROUND) for plane, blur in zip(mates, blurs)]
         mis_e, mis_o = columns([mm(t["row_mid"][...], misfit) for misfit in misfits])
-        cross_e = cross_e + summed_over(times_conj(mis_e, spec_e[at]), half)
-        cross_o = cross_o + summed_over(times_conj(mis_o, spec_o[at]), half)
+        cross_e = cross_e + summed_over(times_conj(mis_e, even), half)
+        cross_o = cross_o + summed_over(times_conj(mis_o, odd), half)
     lagged = join_cols(mm(cross_e * flips, even_back[...]), mm(swapped(cross_o) * turn_off, odd_back[...]))
     psf_grad = mm(t["row_lag_back"][...], lagged)
 
@@ -364,8 +364,26 @@
             device_id=across(jnp.where(lowest, near, 0) + step, to_lane), device_id_type=MESH,
         )
 
+    def spot_send(off):
+        return pltpu.make_async_remote_copy(
+            spot_sum, spots.at[spot], s6.at[off - 1], r6.at[off - 1],
+            device_id=at_spot(off), device_id_type=MESH,
+        )
+
+    def window(which):
+        for first in groups:
+            even, odd = columns(
+                [mm(t["row_all"][...], big[plane, pl.ds(which * rows, span)]) for plane in range(first, first + GROUP)]
+            )
+            spec_e[which, pl.ds(first * half, GROUP * half)] = even
+            spec_o[which, pl.ds(first * half, GROUP * half)] = odd
+
     for off in range(1, RING):
         scatter(off).start()
+    for first in groups:
+        wait_group(halo2, first)
+    for first in groups:
+        wait_group(halo3, first)
     for off in range(1, RING):
         scatter(off).wait()
     summed = share[spot]
@@ -375,6 +393,7 @@
     for off in range(1, slabs):
         exchange(off).start()
     stack[slab] = summed
+    window(0)
     for off in range(1, slabs):
         exchange(off).wait()
     summed = stack[0]
@@ -383,10 +402,7 @@
     full[spot] = summed
     for off in range(1, RING):
         gather(off).start()
-    for off in range(1, RING):
-        gather(off).wait()
-    gradient = jnp.concatenate([full[piece] for piece in range(RING)], axis=0)
-    square[...] = jnp.broadcast_to(jnp.sum(gradient * gradient), (8, 128))
+    square[...] = jnp.broadcast_to(jnp.sum(summed * summed), (8, 128))
     for off in range(1, lanes):
         lane_sum(off).start()
 
@@ -397,11 +413,19 @@
                 far_sum(step, to_lane).start()
 
     sums[layer] = square[...]
+    window(1)
     for off in range(1, depths):
         other = lax.rem(layer + off, depths)
         pltpu.make_async_remote_copy(
             sums.at[other], sums.at[other], s4.at[0], r4.at[other], device_id=at_lane(1), device_id_type=MESH
         ).wait_recv()
+    squares = sums[0]
+    for other in range(1, depths):
+        squares = squares + sums[other]
+    spot_sum[...] = squares
+    for off in range(1, RING):
+        spot_send(off).start()
+    spots[spot] = squares
     for off in range(1, lanes):
         lane_sum(off).wait_send()
 
@@ -411,27 +435,34 @@
             for to_lane in range(lanes):
                 far_sum(step, to_lane).wait_send()
 
-    squares = sums[0]
-    for other in range(1, depths):
-        squares = squares + sums[other]
+    for off in range(1, RING):
+        gather(off).wait()
+    gradient = jnp.concatenate([full[piece] for piece in range(RING)], axis=0)
+    for off in range(1, RING):
+        spot_send(off).wait()
+    squares = spots[0]
+    for other in range(1, RING):
+        squares = squares + spots[other]
     mean_square = squares[0:1] * (1.0 / (depths * PUP * PUP))
     new_phase = phase - STEP_SIZE * gradient / jnp.sqrt(mean_square + EPSILON)
     out_phase[...] = new_phase
 
     _, _, _, total, intensity = spread_of(new_phase)
     kernel_e, kernel_o = spectrum_of(intensity, total)
+    twice_e, twice_o = twice(kernel_e), twice(kernel_o)
     for first in groups:
-        for plane, blur in zip(range(first, first + GROUP), blurred(first, kernel_e, kernel_o)):
-            rstrip[plane, pl.ds(HALF, rows)] = obs[plane] / (blur + BACKGROUND)
-            halo2(plane, 0).start()
-            halo2(plane, 1).start()
-    for first in groups:
-        wait_group(halo2, first)
         mates = range(first, first + GROUP)
-        even, odd = columns([mm(t["row_all"][...], rstrip[plane]) for plane in mates])
-        corrections = back(times_conj(even, twice(kernel_e)), times_conj(odd, twice(kernel_o)))
+        at = pl.ds(first * half, GROUP * half)
+        ratios = []
+        for which in range(2):
+            blurs = back(times(spec_e[which, at], twice_e), times(spec_o[which, at], twice_o))
+            ratios.append(
+                [obs[plane, pl.ds(which * rows, rows)] / (blur + BACKGROUND) for plane, blur in zip(mates, blurs)]
+            )
+        even, odd = columns([mm(t["row_all"][...], above(one, two)) for one, two in zip(*ratios)])
+        corrections = back(times_conj(even, twice_e), times_conj(odd, twice_o))
         for plane, correction in zip(mates, corrections):
-            out_obj[plane] = strip[plane, pl.ds(HALF, rows)] * correction
+            out_obj[plane] = big[plane, pl.ds(rows, rows)] * correction
 
 
 def write_kernel(objects, phase, objects_out, phase_out, sem):
@@ -466,16 +497,15 @@
         out_specs=(pl.BlockSpec(memory_space=vmem), pl.BlockSpec(memory_space=vmem)),
         scratch_shapes=[vmem(table[name].shape, f32) for name in NAMES]
         + [
-            vmem((planes, rows, cols), f32),
             vmem((PUP, PUP), f32),
             vmem((PUP, PUP), f32),
             dma((4 + len(NAMES),)),
             vmem((cols, cols), f32),
             vmem((cols, cols), f32),
+            vmem((planes, 3 * rows, cols), f32),
             vmem((planes, span, cols), f32),
-            vmem((planes, span, cols), f32),
-            vmem((planes * half, cols), f32),
-            vmem((planes * half, cols), f32),
+            vmem((2, planes * half, cols), f32),
+            vmem((2, planes * half, cols), f32),
             vmem((RING, chunk, PUP), f32),
             vmem((RING - 1, chunk, PUP), f32),
             vmem((chunk, PUP), f32),
@@ -483,10 +513,12 @@
             vmem((RING, chunk, PUP), f32),
             vmem((8, 128), f32),
             vmem((depths, 8, 128), f32),
-            dma((2 * planes,)), dma((2 * planes,)), dma((2 * planes,)), dma((2 * planes,)),
+            vmem((RING, 8, 128), f32),
+            vmem((8, 128), f32),
+            dma((2 * planes,)), dma((2 * planes,)), dma((2 * planes,)), dma((2 * planes,)), dma((2 * planes,)), dma((2 * planes,)),
             dma((RING - 1,)), dma((RING - 1,)), dma((slabs - 1,)), dma((slabs - 1,)),
             dma((RING - 1,)), dma((RING - 1,)), dma((lanes - 1,)), dma((depths,)),
-            dma((slabs // 2 * lanes,)),
+            dma((slabs // 2 * lanes,)), dma((RING - 1,)), dma((RING - 1,)),
         ],
         compiler_params=pltpu.CompilerParams(
             collective_id=0, has_side_effects=True, vmem_limit_bytes=48 * 1024 * 1024

time: 46.3 us -> 44.3 us (0.957)
  Pallas kernels: 45.5 us -> 43.5 us
    pallas_call x1, Pallas kernels: 44.7 us -> 42.7 us  [on_device(): pl.pallas_call(body, out_shape=(jax.ShapeDtypeStruct((planes, rows, cols)...]
where the time goes in v4:
time: 44.3 us; the launch traced here: 44.2 us
  Pallas kernels  43.5 us (98%)
  between operations  0.64 us (1%)
    pallas_call x1, Pallas kernels, on_device(): pl.pallas_call(body, out_shape=(jax.ShapeDtypeStruct((planes, rows, cols)...  42.7 us

profile of v4, /device:TPU:1, one launch (start us, length us, event | category | flops | bytes accessed | tf_op | source)
XLA Modules:
  0.0 44.2 jit_solution(1868154271938385243)
XLA Ops:
  0.6 42.7 %step.1 = (f32[4,128,256]{2,1,0:T(8,128)S(1)}, f32[128,128]{1,0:T(8,128)S(1)}) custom-call(f32[4,128,256]{2,1,0:T(8,128)} %bitcast.6, f32[4,128,256]{2,1,0:T(8,128)} %bitcast.7, f32[128,128]{1,0:T(8,128)} %bitcast.8, f32[128,128]{1,0:T(8,128)} %bitcast.9, f32[128,128]{1,0:T(8,128)} %constant.20.clone.refs_4_, f32[272,128]{1,0:T(8,128)} %constant.21.clone.refs_5_, ...), custom_call_target="tpu_custom_call" | custom-call | tf_op jit(solution)/shard_map/step/pallas_call | solution.py:490
  43.4 0.8 %write.1 = (f32[4,128,256]{2,1,0:T(8,128)}, f32[128,128]{1,0:T(8,128)}) custom-call(f32[4,128,256]{2,1,0:T(8,128)S(1)} %get-tuple-element.6.objects, f32[128,128]{1,0:T(8,128)S(1)} %get-tuple-element.7.phase), custom_call_target="tpu_custom_call" | custom-call | tf_op jit(solution)/shard_map/write/pallas_call | solution.py:531

commit v5 on v4

--- a/solution.py
+++ b/solution.py
@@ -294,13 +294,7 @@
     for plane in range(planes):
         halo1(plane, 0).start()
         halo1(plane, 1).start()
-    for plane in range(planes):
-        halo2(plane, 0).start()
-        halo2(plane, 1).start()
     ready(*[name for name in loads if name not in EARLY])
-    for plane in range(planes):
-        halo3(plane, 0).start()
-        halo3(plane, 1).start()
     even_back[...] = t["even"][...].T
     odd_back[...] = t["odd"][...].T
     kernel_e, kernel_o = spectrum_of(intensity, total)
@@ -380,10 +374,9 @@
 
     for off in range(1, RING):
         scatter(off).start()
-    for first in groups:
-        wait_group(halo2, first)
-    for first in groups:
-        wait_group(halo3, first)
+    for plane in range(planes):
+        halo2(plane, 0).start()
+        halo2(plane, 1).start()
     for off in range(1, RING):
         scatter(off).wait()
     summed = share[spot]
@@ -393,7 +386,9 @@
     for off in range(1, slabs):
         exchange(off).start()
     stack[slab] = summed
-    window(0)
+    for plane in range(planes):
+        halo3(plane, 0).start()
+        halo3(plane, 1).start()
     for off in range(1, slabs):
         exchange(off).wait()
     summed = stack[0]
@@ -413,6 +408,9 @@
                 far_sum(step, to_lane).start()
 
     sums[layer] = square[...]
+    for first in groups:
+        wait_group(halo2, first)
+    window(0)
     window(1)
     for off in range(1, depths):
         other = lax.rem(layer + off, depths)
@@ -438,6 +436,8 @@
     for off in range(1, RING):
         gather(off).wait()
     gradient = jnp.concatenate([full[piece] for piece in range(RING)], axis=0)
+    for first in groups:
+        wait_group(halo3, first)
     for off in range(1, RING):
         spot_send(off).wait()
     squares = spots[0]
@@ -449,10 +449,10 @@
 
     _, _, _, total, intensity = spread_of(new_phase)
     kernel_e, kernel_o = spectrum_of(intensity, total)
-    twice_e, twice_o = twice(kernel_e), twice(kernel_o)
-    for first in groups:
-        mates = range(first, first + GROUP)
-        at = pl.ds(first * half, GROUP * half)
+    twice_e, twice_o = stacked([kernel_e] * planes), stacked([kernel_o] * planes)
+    for first in range(0, planes, planes):
+        mates = range(first, first + planes)
+        at = pl.ds(first * half, planes * half)
         ratios = []
         for which in range(2):
             blurs = back(times(spec_e[which, at], twice_e), times(spec_o[which, at], twice_o))

time: 44.3 us -> 43.6 us (0.984)
  Pallas kernels: 43.5 us -> 42.9 us
    pallas_call x1, Pallas kernels: 42.7 us -> 42 us  [on_device(): pl.pallas_call(body, out_shape=(jax.ShapeDtypeStruct((planes, rows, cols)...]
where the time goes in v5:
time: 43.6 us; the launch traced here: 43.5 us
  Pallas kernels  42.9 us (98%)
  between operations  0.64 us (1%)
    pallas_call x1, Pallas kernels, on_device(): pl.pallas_call(body, out_shape=(jax.ShapeDtypeStruct((planes, rows, cols)...  42 us

profile of v5, /device:TPU:1, one launch (start us, length us, event | category | flops | bytes accessed | tf_op | source)
XLA Modules:
  0.0 43.5 jit_solution(6747414975693303512)
XLA Ops:
  0.6 42.0 %step.1 = (f32[4,128,256]{2,1,0:T(8,128)S(1)}, f32[128,128]{1,0:T(8,128)S(1)}) custom-call(f32[4,128,256]{2,1,0:T(8,128)} %bitcast.6, f32[4,128,256]{2,1,0:T(8,128)} %bitcast.7, f32[128,128]{1,0:T(8,128)} %bitcast.8, f32[128,128]{1,0:T(8,128)} %bitcast.9, f32[128,128]{1,0:T(8,128)} %constant.20.clone.refs_4_, f32[272,128]{1,0:T(8,128)} %constant.21.clone.refs_5_, ...), custom_call_target="tpu_custom_call" | custom-call | tf_op jit(solution)/shard_map/step/pallas_call | solution.py:490
  42.7 0.8 %write.1 = (f32[4,128,256]{2,1,0:T(8,128)}, f32[128,128]{1,0:T(8,128)}) custom-call(f32[4,128,256]{2,1,0:T(8,128)S(1)} %get-tuple-element.6.objects, f32[128,128]{1,0:T(8,128)S(1)} %get-tuple-element.7.phase), custom_call_target="tpu_custom_call" | custom-call | tf_op jit(solution)/shard_map/write/pallas_call | solution.py:531

commit v6 on v5

--- a/solution.py
+++ b/solution.py
@@ -133,7 +133,7 @@
 
 
 NAMES = ("aperture", "left", "right", "row_lag", "row_all", "even", "odd", "row_back", "row_mid", "row_lag_back")
-EARLY = ("phase", "amp", "aperture", "left", "right", "obj")
+EARLY = ("left", "right", "phase", "amp", "aperture", "obj")
 
 
 def kernel(tiles, depths, planes, rows, cols, *refs):
@@ -143,7 +143,7 @@
     out_obj, out_phase = refs[4 + count : 6 + count]
     t = dict(zip(NAMES, refs[6 + count : 6 + 2 * count]))
     (
-        phase_ref, amp_ref, load_sem, even_back, odd_back, big, obs, spec_e, spec_o,
+        phase_ref, amp_ref, load_sem, left_full, right_full, even_back, odd_back, big, obs, spec_e, spec_o,
         share, part, mine, stack, full, square, sums, spots, spot_sum,
         h1s, h1r, h2s, h2r, h3s, h3r, s1, r1, s2, r2, s3, r3, s4, r4, s5, s6, r6,
     ) = refs[6 + 2 * count :]
@@ -179,16 +179,16 @@
     def greet(device):
         pl.semaphore_signal(barrier, 1, device_id=device, device_id_type=MESH)
 
+    for to_lane in range(lanes):
+        greet(across(source_slab, to_lane))
     greet(at_tile(lax.rem(me + 1, tiles)))
     greet(at_tile(lax.rem(me + tiles - 1, tiles)))
-    for off in range(1, RING):
-        greet(at_spot(off))
     for off in range(1, slabs):
         greet(at_slab(off))
     for off in range(1, lanes):
         greet(at_lane(off))
-    for to_lane in range(lanes):
-        greet(across(source_slab, to_lane))
+    for off in range(1, RING):
+        greet(at_spot(off))
     near_sends = jnp.where(lowest | highest, near * lanes, 0)
     greeted = 2 + RING - 1 + slabs - 1 + lanes - 1 + near_sends
 
@@ -225,20 +225,18 @@
     def halo3(plane, direction):
         return halo(obs, HALF, *((rows - HALF, -HALF) if direction == 0 else (0, rows)), h3s, h3r, plane, direction)
 
-    def full_left():
+    def build_pupil():
         real, imag = t["left"][:PAD], t["left"][PAD:]
-        return above(beside(real, -imag), beside(imag, real))
-
-    def full_right():
+        left_full[...] = above(beside(real, -imag), beside(imag, real))
         real, imag = t["right"][:PUP], t["right"][PUP:]
-        return above(beside(real, imag), beside(-imag, real))
+        right_full[...] = above(beside(real, imag), beside(-imag, real))
 
     def spread_of(angle):
         sine, cosine = sin_cos(angle)
         weight = amp_ref[...] * t["aperture"][...]
         field = above(weight * cosine, weight * sine)
-        lefts = mm(full_left(), field)
-        outer = mm(beside(lefts[:PAD], lefts[PAD:]), full_right())
+        lefts = mm(left_full[...], field)
+        outer = mm(beside(lefts[:PAD], lefts[PAD:]), right_full[...])
         real, imag = outer[:, :cols], outer[:, cols:]
         intensity = real * real + imag * imag
         total = jnp.sum(intensity)
@@ -286,7 +284,9 @@
             halo_of(plane, 0).wait()
             halo_of(plane, 1).wait()
 
-    ready("phase", "amp", "aperture", "left", "right")
+    ready("left", "right")
+    build_pupil()
+    ready("phase", "amp", "aperture")
     phase = phase_ref[...]
     field, real, imag, total, intensity = spread_of(phase)
     ready("obj")
@@ -316,7 +316,7 @@
     scale = 2.0 / total
     centred = (psf_grad - jnp.sum(psf_grad * intensity) / total) * scale
     rest = jnp.zeros((cols - PAD, cols), jnp.float32)
-    right = full_right()
+    right = right_full[...]
     lefts = mm(right, jnp.concatenate([centred * real, rest, centred * imag, rest], axis=0))
     pupils = lax.dot_general(
         beside(lefts[:PUP], lefts[PUP:]), right, (((1,), (1,)), ((), ())),
@@ -397,7 +397,7 @@
     full[spot] = summed
     for off in range(1, RING):
         gather(off).start()
-    square[...] = jnp.broadcast_to(jnp.sum(summed * summed), (8, 128))
+    square[...] = jnp.broadcast_to(jnp.sum(summed * summed), (1, 128))
     for off in range(1, lanes):
         lane_sum(off).start()
 
@@ -443,7 +443,7 @@
     squares = spots[0]
     for other in range(1, RING):
         squares = squares + spots[other]
-    mean_square = squares[0:1] * (1.0 / (depths * PUP * PUP))
+    mean_square = squares * (1.0 / (depths * PUP * PUP))
     new_phase = phase - STEP_SIZE * gradient / jnp.sqrt(mean_square + EPSILON)
     out_phase[...] = new_phase
 
@@ -500,6 +500,8 @@
             vmem((PUP, PUP), f32),
             vmem((PUP, PUP), f32),
             dma((4 + len(NAMES),)),
+            vmem((2 * PAD, 2 * PUP), f32),
+            vmem((2 * PUP, 2 * cols), f32),
             vmem((cols, cols), f32),
             vmem((cols, cols), f32),
             vmem((planes, 3 * rows, cols), f32),
@@ -511,10 +513,10 @@
             vmem((chunk, PUP), f32),
             vmem((slabs, chunk, PUP), f32),
             vmem((RING, chunk, PUP), f32),
-            vmem((8, 128), f32),
-            vmem((depths, 8, 128), f32),
-            vmem((RING, 8, 128), f32),
-            vmem((8, 128), f32),
+            vmem((1, 128), f32),
+            vmem((depths, 1, 128), f32),
+            vmem((RING, 1, 128), f32),
+            vmem((1, 128), f32),
             dma((2 * planes,)), dma((2 * planes,)), dma((2 * planes,)), dma((2 * planes,)), dma((2 * planes,)), dma((2 * planes,)),
             dma((RING - 1,)), dma((RING - 1,)), dma((slabs - 1,)), dma((slabs - 1,)),
             dma((RING - 1,)), dma((RING - 1,)), dma((lanes - 1,)), dma((depths,)),

time: 43.6 us -> 43.4 us (level)
  no operation moved by 1% of the time
where the time goes in v6:
time: 43.4 us; the launch traced here: 43.3 us
  Pallas kernels  42.6 us (98%)
  between operations  0.64 us (1%)
    pallas_call x1, Pallas kernels, on_device(): pl.pallas_call(body, out_shape=(jax.ShapeDtypeStruct((planes, rows, cols)...  41.8 us

profile of v6, /device:TPU:1, one launch (start us, length us, event | category | flops | bytes accessed | tf_op | source)
XLA Modules:
  0.0 43.3 jit_solution(8951505853300430423)
XLA Ops:
  0.6 41.8 %step.1 = (f32[4,128,256]{2,1,0:T(8,128)S(1)}, f32[128,128]{1,0:T(8,128)S(1)}) custom-call(f32[4,128,256]{2,1,0:T(8,128)} %bitcast.6, f32[4,128,256]{2,1,0:T(8,128)} %bitcast.7, f32[128,128]{1,0:T(8,128)} %bitcast.8, f32[128,128]{1,0:T(8,128)} %bitcast.9, f32[128,128]{1,0:T(8,128)} %constant.20.clone.refs_4_, f32[272,128]{1,0:T(8,128)} %constant.21.clone.refs_5_, ...), custom_call_target="tpu_custom_call" | custom-call | tf_op jit(solution)/shard_map/step/pallas_call | solution.py:490
  42.5 0.8 %write.1 = (f32[4,128,256]{2,1,0:T(8,128)}, f32[128,128]{1,0:T(8,128)}) custom-call(f32[4,128,256]{2,1,0:T(8,128)S(1)} %get-tuple-element.6.objects, f32[128,128]{1,0:T(8,128)S(1)} %get-tuple-element.7.phase), custom_call_target="tpu_custom_call" | custom-call | tf_op jit(solution)/shard_map/write/pallas_call | solution.py:533

commit v7 on v6

--- a/solution.py
+++ b/solution.py
@@ -364,8 +364,9 @@
             device_id=at_spot(off), device_id_type=MESH,
         )
 
-    def window(which):
-        for first in groups:
+    def windows(first):
+        wait_group(halo2, first)
+        for which in range(2):
             even, odd = columns(
                 [mm(t["row_all"][...], big[plane, pl.ds(which * rows, span)]) for plane in range(first, first + GROUP)]
             )
@@ -374,9 +375,6 @@
 
     for off in range(1, RING):
         scatter(off).start()
-    for plane in range(planes):
-        halo2(plane, 0).start()
-        halo2(plane, 1).start()
     for off in range(1, RING):
         scatter(off).wait()
     summed = share[spot]
@@ -386,6 +384,9 @@
     for off in range(1, slabs):
         exchange(off).start()
     stack[slab] = summed
+    for plane in range(planes):
+        halo2(plane, 0).start()
+        halo2(plane, 1).start()
     for plane in range(planes):
         halo3(plane, 0).start()
         halo3(plane, 1).start()
@@ -408,10 +409,7 @@
                 far_sum(step, to_lane).start()
 
     sums[layer] = square[...]
-    for first in groups:
-        wait_group(halo2, first)
-    window(0)
-    window(1)
+    windows(0)
     for off in range(1, depths):
         other = lax.rem(layer + off, depths)
         pltpu.make_async_remote_copy(
@@ -424,6 +422,8 @@
     for off in range(1, RING):
         spot_send(off).start()
     spots[spot] = squares
+    for first in groups[1:]:
+        windows(first)
     for off in range(1, lanes):
         lane_sum(off).wait_send()
 

time: 43.4 us -> 42.8 us (0.986)
  Pallas kernels: 42.6 us -> 42 us
    pallas_call x1, Pallas kernels: 41.8 us -> 41.2 us  [on_device(): pl.pallas_call(body, out_shape=(jax.ShapeDtypeStruct((planes, rows, cols)...]
where the time goes in v7:
time: 42.8 us; the launch traced here: 42.7 us
  Pallas kernels  42 us (98%)
  between operations  0.64 us (1%)
    pallas_call x1, Pallas kernels, on_device(): pl.pallas_call(body, out_shape=(jax.ShapeDtypeStruct((planes, rows, cols)...  41.2 us

profile of v7, /device:TPU:1, one launch (start us, length us, event | category | flops | bytes accessed | tf_op | source)
XLA Modules:
  0.0 42.7 jit_solution(13822951924095709293)
XLA Ops:
  0.6 41.2 %step.1 = (f32[4,128,256]{2,1,0:T(8,128)S(1)}, f32[128,128]{1,0:T(8,128)S(1)}) custom-call(f32[4,128,256]{2,1,0:T(8,128)} %bitcast.6, f32[4,128,256]{2,1,0:T(8,128)} %bitcast.7, f32[128,128]{1,0:T(8,128)} %bitcast.8, f32[128,128]{1,0:T(8,128)} %bitcast.9, f32[128,128]{1,0:T(8,128)} %constant.20.clone.refs_4_, f32[272,128]{1,0:T(8,128)} %constant.21.clone.refs_5_, ...), custom_call_target="tpu_custom_call" | custom-call | tf_op jit(solution)/shard_map/step/pallas_call | solution.py:490
  41.8 0.8 %write.1 = (f32[4,128,256]{2,1,0:T(8,128)}, f32[128,128]{1,0:T(8,128)}) custom-call(f32[4,128,256]{2,1,0:T(8,128)S(1)} %get-tuple-element.6.objects, f32[128,128]{1,0:T(8,128)S(1)} %get-tuple-element.7.phase), custom_call_target="tpu_custom_call" | custom-call | tf_op jit(solution)/shard_map/write/pallas_call | solution.py:533

commit v8 on v7

--- a/solution.py
+++ b/solution.py
@@ -387,9 +387,6 @@
     for plane in range(planes):
         halo2(plane, 0).start()
         halo2(plane, 1).start()
-    for plane in range(planes):
-        halo3(plane, 0).start()
-        halo3(plane, 1).start()
     for off in range(1, slabs):
         exchange(off).wait()
     summed = stack[0]
@@ -408,6 +405,9 @@
             for to_lane in range(lanes):
                 far_sum(step, to_lane).start()
 
+    for plane in range(planes):
+        halo3(plane, 0).start()
+        halo3(plane, 1).start()
     sums[layer] = square[...]
     windows(0)
     for off in range(1, depths):

time: 42.8 us -> 42.8 us (level)
  no operation moved by 1% of the time
where the time goes in v8:
time: 42.8 us; the launch traced here: 42.7 us
  Pallas kernels  42 us (98%)
  between operations  0.64 us (1%)
    pallas_call x1, Pallas kernels, on_device(): pl.pallas_call(body, out_shape=(jax.ShapeDtypeStruct((planes, rows, cols)...  41.2 us

profile of v8, /device:TPU:1, one launch (start us, length us, event | category | flops | bytes accessed | tf_op | source)
XLA Modules:
  0.0 42.7 jit_solution(8115462698696581084)
XLA Ops:
  0.6 41.2 %step.1 = (f32[4,128,256]{2,1,0:T(8,128)S(1)}, f32[128,128]{1,0:T(8,128)S(1)}) custom-call(f32[4,128,256]{2,1,0:T(8,128)} %bitcast.6, f32[4,128,256]{2,1,0:T(8,128)} %bitcast.7, f32[128,128]{1,0:T(8,128)} %bitcast.8, f32[128,128]{1,0:T(8,128)} %bitcast.9, f32[128,128]{1,0:T(8,128)} %constant.20.clone.refs_4_, f32[272,128]{1,0:T(8,128)} %constant.21.clone.refs_5_, ...), custom_call_target="tpu_custom_call" | custom-call | tf_op jit(solution)/shard_map/step/pallas_call | solution.py:490
  41.8 0.8 %write.1 = (f32[4,128,256]{2,1,0:T(8,128)}, f32[128,128]{1,0:T(8,128)}) custom-call(f32[4,128,256]{2,1,0:T(8,128)S(1)} %get-tuple-element.6.objects, f32[128,128]{1,0:T(8,128)S(1)} %get-tuple-element.7.phase), custom_call_target="tpu_custom_call" | custom-call | tf_op jit(solution)/shard_map/write/pallas_call | solution.py:533
